TPU v7x, 512 devices: a whole 4x8x8 slice. The times are simulated.
512 devices in a mesh: row: 32 (over x, z), col: 16 (over y, core).
Axes of the slice: x: 4, y: 8, z: 8, core: 2. Of those that a mesh axis runs over, the one named last changes fastest.
Arguments:
- basis_now: float32 [131072, 128], P(('row', 'col')), may hold values from -6 to 6
- basis_prev: float32 [131072, 128], P(('row', 'col')), may hold values from -6 to 6
- coupling: float32 [128, 128], replicated, may hold values from -0.875 to 0.875
- tiles: bfloat16 [32, 16, 16, 128, 128], P('row', 'col'), may hold values from -0.1875 to 0.1875
- tile_rows: int32 [32, 16, 16], P('row', 'col'), may hold values from 0 to 63
- tile_cols: int32 [32, 16, 16], P('row', 'col'), may hold values from 0 to 31
- tile_counts: int32 [32, 16], P('row', 'col'), may hold values from 4 to 16, as said below
Outputs:
- basis: float32 [131072, 128], P(('row', 'col'))
- projection: float32 [128, 128], replicated
- rfactor: float32 [128, 128], replicated
Inputs may be any that keep to these rules, and one draw needn't show every extreme that they name: Each device uses the first tile_counts of its 16 tile slots; some device uses all of them.
All inputs are finite; a program needn't handle non-finite values.
Results may differ from a plain program's by a relative error of at most 0.0033.
Values may be sent and summed in bfloat16 or wider, within the bound.
A program may use at most 64 MiB of HBM per device.

v0:
```python
import jax
import jax.numpy as jnp
from jax import lax
from jax.sharding import PartitionSpec as P

HIGHEST = lax.Precision.HIGHEST


def swapped(value, axis, bit):
    return lax.ppermute(value, axis, [(i, i ^ 1 << bit) for i in range(lax.axis_size(axis))])


def inner_product(left, right):
    return jnp.dot(left.T, right, precision=HIGHEST)


def upper_cholesky(gram):
    return jnp.linalg.cholesky(gram).T


def lower_inverse(lower_part):
    identity = jnp.eye(lower_part.shape[0], dtype=lower_part.dtype)
    return jax.scipy.linalg.solve_triangular(lower_part, identity, lower=True)


def on_device(basis_now, basis_prev, coupling, tiles, tile_rows, tile_cols, tile_counts):
    rows_dev, block_width = basis_now.shape
    tile_block = tiles[0, 0]
    row_ids = tile_rows[0, 0]
    col_ids = tile_cols[0, 0]
    tile_total = tile_counts[0, 0]
    tile_size = tile_block.shape[-1]
    slot_count = tile_block.shape[0]
    half_basis = basis_now.astype(jnp.bfloat16)
    gathered = lax.all_gather(half_basis, "col", axis=0, tiled=True)
    stacked = gathered.reshape(-1, tile_size, block_width)
    chosen = jnp.take(stacked, col_ids, axis=0)
    products = jnp.einsum("tij,tjb->tib", tile_block, chosen, preferred_element_type=jnp.float32)
    usable = jnp.arange(slot_count) < tile_total
    row_tiles = lax.axis_size("row") * rows_dev // tile_size
    selector = (row_ids[None, :] == jnp.arange(row_tiles)[:, None]) & usable[None, :]
    combined = jnp.einsum("rt,tib->rib", selector.astype(jnp.float32), products, precision=HIGHEST)
    product = lax.psum_scatter(
        combined.reshape(row_tiles * tile_size, block_width), "row", scatter_dimension=0, tiled=True
    )
    device_count = lax.axis_size("row") * lax.axis_size("col")
    total_rows = float(rows_dev * device_count)
    norm_scale = total_rows ** (-0.5)
    upper_part = jnp.triu(coupling)
    pieces = (inner_product(basis_now, product),)
    totals = lax.psum((pieces[0],), ("row", "col"))
    projection = totals[0] * norm_scale
    residual = product - jnp.dot(basis_now, projection, precision=HIGHEST) * norm_scale
    residual = residual - jnp.dot(basis_prev, upper_part.T, precision=HIGHEST)
    levels = device_count.bit_length() - 1
    factor_mine = residual
    for level in range(levels):
        factor_other = swapped(factor_mine, ("row", "col"), level)
        gram = inner_product(factor_mine, factor_mine) + inner_product(factor_other, factor_other)
        factor_mine = upper_cholesky(gram)
    rfactor = factor_mine * norm_scale
    inverse = lower_inverse(rfactor.T)
    basis = jnp.dot(residual, inverse.T, precision=HIGHEST)
    return (basis, projection, rfactor)


def solution(mesh):
    placed = (
        P(("row", "col"), None),
        P(("row", "col"), None),
        P(),
        P("row", "col", None, None, None),
        P("row", "col", None),
        P("row", "col", None),
        P("row", "col"),
    )
    return jax.shard_map(
        on_device,
        mesh=mesh,
        in_specs=placed,
        out_specs=(P(("row", "col"), None), P(), P()),
        check_vma=False,
    )
```

profile of v0, /device:TPU:2, one launch (start us, length us, event | category | flops | bytes accessed | tf_op | source)
XLA Modules:
  0.0 774.7 jit_solution(17819129505107521750)
XLA Ops:
  10.9 45.2 %all-gather.2.cloned.1.call-done = bf16[4096,128]{1,0:T(8,128)(2,1)} async-done(((bf16[256,128]{1,0:T(8,128)(2,1)}), bf16[4096,128]{1,0:T(8,128)(2,1)}) %all-gather.2.cloned.1.call-update) | async-done | bytes 1048592 | tf_op jit(solution)/shard_map/all_gather | solution.py:35
  61.1 4.4 copy.39
  65.5 5.6 copy.40
  71.2 229.1 %reduce-scatter.2.cloned.1.call-done = f32[256,128]{0,1:T(8,128)} async-done(((f32[8192,128]{0,1:T(8,128)}), f32[256,128]{0,1:T(8,128)}) %reduce-scatter.2.cloned.1.call-update) | async-done | bytes 131088 | tf_op jit(solution)/shard_map/reduce_scatter | solution.py:43
  302.3 260.6 %all-reduce.2.cloned.1.call-done = f32[128,128]{1,0:T(8,128)} async-done(((f32[128,128]{1,0:T(8,128)}), f32[128,128]{1,0:T(8,128)}) %all-reduce.2.cloned.1.call-update) | async-done | bytes 65552 | tf_op jit(solution)/shard_map/psum | solution.py:51
  565.3 6.4 collective-permute-start
  573.1 11.7 %cholesky.149 = f32[128,128]{1,0:T(8,128)S(1)} custom-call(f32[128,128]{1,0:T(8,128)S(1)} %fusion.20), custom_call_target="Cholesky" | custom-call | tf_op jit(solution)/shard_map/jit(cholesky)/cholesky | solution.py:18
  586.2 3.3 collective-permute-start.1
  592.8 11.7 %cholesky.160 = f32[128,128]{1,0:T(8,128)S(1)} custom-call(f32[128,128]{1,0:T(8,128)S(1)} %fusion.19), custom_call_target="Cholesky" | custom-call | tf_op jit(solution)/shard_map/jit(cholesky)/cholesky | solution.py:18
  605.9 3.2 collective-permute-start.2
  610.0 3.7 collective-permute-done.2
  614.0 11.7 %cholesky.171 = f32[128,128]{1,0:T(8,128)S(1)} custom-call(f32[128,128]{1,0:T(8,128)S(1)} %fusion.18), custom_call_target="Cholesky" | custom-call | tf_op jit(solution)/shard_map/jit(cholesky)/cholesky | solution.py:18
  630.8 6.7 collective-permute-done.3
  637.8 11.7 %cholesky.182 = f32[128,128]{1,0:T(8,128)S(1)} custom-call(f32[128,128]{1,0:T(8,128)S(1)} %fusion.17), custom_call_target="Cholesky" | custom-call | tf_op jit(solution)/shard_map/jit(cholesky)/cholesky | solution.py:18
  657.4 11.7 %cholesky.193 = f32[128,128]{1,0:T(8,128)S(1)} custom-call(f32[128,128]{1,0:T(8,128)S(1)} %fusion.16), custom_call_target="Cholesky" | custom-call | tf_op jit(solution)/shard_map/jit(cholesky)/cholesky | solution.py:18
  674.3 4.0 collective-permute-done.5
  678.6 11.7 %cholesky.204 = f32[128,128]{1,0:T(8,128)S(1)} custom-call(f32[128,128]{1,0:T(8,128)S(1)} %fusion.15), custom_call_target="Cholesky" | custom-call | tf_op jit(solution)/shard_map/jit(cholesky)/cholesky | solution.py:18
  694.5 7.2 collective-permute-done.6
  702.2 11.7 %cholesky.215 = f32[128,128]{1,0:T(8,128)S(1)} custom-call(f32[128,128]{1,0:T(8,128)S(1)} %fusion.14), custom_call_target="Cholesky" | custom-call | tf_op jit(solution)/shard_map/jit(cholesky)/cholesky | solution.py:18
  721.8 11.7 %cholesky.226 = f32[128,128]{1,0:T(8,128)S(1)} custom-call(f32[128,128]{1,0:T(8,128)S(1)} %fusion.13), custom_call_target="Cholesky" | custom-call | tf_op jit(solution)/shard_map/jit(cholesky)/cholesky | solution.py:18
  734.8 3.2 collective-permute-start.8
  738.9 3.5 collective-permute-done.8
  742.9 11.7 %cholesky.237 = f32[128,128]{1,0:T(8,128)S(1)} custom-call(f32[128,128]{1,0:T(8,128)S(1)} %fusion.12), custom_call_target="Cholesky" | custom-call | tf_op jit(solution)/shard_map/jit(cholesky)/cholesky | solution.py:18
  755.9 9.8 %custom-call.6 = f32[1,128,128]{1,2,0:T(8,128)S(1)} custom-call(f32[1,128,128]{2,1,0:T(8,128)S(1)} %get-tuple-element.11), custom_call_target="InvertDiagBlocksLowerTriangular" | custom-call | tf_op jit(solution)/shard_map/jit(_solve_triangular)/triangular_solve | solution.py:23
  (107 shorter events, 58.1 us)
Async XLA Ops:
  7.2 50.8 %copy-start = (bf16[1,1,16,128,128]{4,3,2,1,0:T(8,128)(2,1)S(1)}, bf16[1,1,16,128,128]{4,3,2,1,0:T(8,128)(2,1)}, u32[]{:S(2)}) copy-start(bf16[1,1,16,128,128]{4,3,2,1,0:T(8,128)(2,1)} %param.11) | copy-start | bytes 1572868
  7.2 52.0 %copy-start.5 = (s32[1,1,16]{2,1,0:T(1,128)S(1)}, s32[1,1,16]{2,1,0:T(1,128)}, u32[]{:S(2)}) copy-start(s32[1,1,16]{2,1,0:T(1,128)} %param.12) | copy-start | bytes 196
  7.2 48.9 %all-gather.2.cloned.1.call-start = ((), (), s32[]{:S(2)}) async-start(), calls=%async_computation.1 | async-start | bytes 1114112 | tf_op jit(solution)/shard_map/all_gather | solution.py:35
  8.8 291.5 %reduce-scatter.2.cloned.1.call-start = ((), (), s32[]{:S(2)}) async-start(), calls=%async_computation.2 | async-start | bytes 4325376 | tf_op jit(solution)/shard_map/reduce_scatter | solution.py:43
  71.1 229.2 %copy-start.1 = (f32[256,128]{1,0:T(8,128)S(1)}, f32[256,128]{1,0:T(8,128)}, u32[]{:S(2)}) copy-start(f32[256,128]{1,0:T(8,128)} %param.8) | copy-start | bytes 393220
  71.1 493.9 %copy-start.3 = (f32[256,128]{1,0:T(8,128)S(1)}, f32[256,128]{1,0:T(8,128)}, u32[]{:S(2)}) copy-start(f32[256,128]{1,0:T(8,128)} %param.9) | copy-start | bytes 393220
  71.1 493.9 %copy-start.4 = (f32[128,128]{1,0:T(8,128)S(1)}, f32[128,128]{1,0:T(8,128)}, u32[]{:S(2)}) copy-start(f32[128,128]{1,0:T(8,128)} %param.10) | copy-start | bytes 196612
  71.2 491.7 %all-reduce.2.cloned.1.call-start = ((), (), s32[]{:S(2)}) async-start(), calls=%async_computation.3 | async-start | bytes 131072 | tf_op jit(solution)/shard_map/psum | solution.py:51
  563.7 158.0 %copy-start.2 = (f32[128,128]{1,0:T(8,128)}, f32[128,128]{1,0:T(8,128)S(1)}, u32[]{:S(2)}) copy-start(f32[128,128]{1,0:T(8,128)S(1)} %broadcast_multiply_fusion) | copy-start | bytes 196612
  565.3 7.4 collective-permute-start
  586.2 6.3 collective-permute-start.1
  605.9 7.8 %collective-permute-start.2 = (f32[128,128]{0,1:T(8,128)S(1)}, f32[128,128]{0,1:T(8,128)S(1)}, u32[]{:S(2)}, u32[]{:S(2)}) collective-permute-start(f32[128,128]{0,1:T(8,128)S(1)} %fusion.40), channel_id=1, source_target_pairs={{0,4},{1,5},{2,6},{3,7},{4,0},{5,1},{6,2},{7,3},{8,12},{9,13},{10,... | collective-permute-start | bytes 196616 | tf_op jit(solution)/shard_map/ppermute | solution.py:10
  627.1 10.4 %collective-permute-start.3 = (f32[128,128]{0,1:T(8,128)S(1)}, f32[128,128]{0,1:T(8,128)S(1)}, u32[]{:S(2)}, u32[]{:S(2)}) collective-permute-start(f32[128,128]{0,1:T(8,128)S(1)} %fusion.42), channel_id=1, source_target_pairs={{0,8},{1,9},{2,10},{3,11},{4,12},{5,13},{6,14},{7,15},{8,0},{9,1},... | collective-permute-start | bytes 196616 | tf_op jit(solution)/shard_map/ppermute | solution.py:10
  650.9 6.2 collective-permute-start.4
  670.5 7.8 %collective-permute-start.5 = (f32[128,128]{0,1:T(8,128)S(1)}, f32[128,128]{0,1:T(8,128)S(1)}, u32[]{:S(2)}, u32[]{:S(2)}) collective-permute-start(f32[128,128]{0,1:T(8,128)S(1)} %fusion.46), channel_id=1, source_target_pairs={{0,32},{1,33},{2,34},{3,35},{4,36},{5,37},{6,38},{7,39},{8,40},{9,... | collective-permute-start | bytes 196616 | tf_op jit(solution)/shard_map/ppermute | solution.py:10
  691.7 10.1 %collective-permute-start.6 = (f32[128,128]{0,1:T(8,128)S(1)}, f32[128,128]{0,1:T(8,128)S(1)}, u32[]{:S(2)}, u32[]{:S(2)}) collective-permute-start(f32[128,128]{0,1:T(8,128)S(1)} %fusion.48), channel_id=1, source_target_pairs={{0,64},{1,65},{2,66},{3,67},{4,68},{5,69},{6,70},{7,71},{8,72},{9,... | collective-permute-start | bytes 196616 | tf_op jit(solution)/shard_map/ppermute | solution.py:10
  715.2 6.2 collective-permute-start.7
  734.8 7.7 collective-permute-start.8
Sparse Core Ops, SparseCore 0:
  10.7 45.3 all-gather.1
  71.3 229.0 reduce-scatter.1
  305.9 256.9 all-reduce.1
where the time goes:
time: 783 us; the launch traced here: 775 us
  waiting for transfers between devices  568 us (73%)
  other arithmetic  131 us (17%)
  starting transfers between devices  28.6 us (4%)
  matrix products  17.3 us (2%)
  between operations  15.3 us (2%)
  local copies, waits for them, and re-layouts  14 us (2%)
    psum x1, waiting for transfers between devices, on_device(): totals = lax.psum((pieces[0],), ('row', 'col'))  261 us
    reduce_scatter x1, waiting for transfers between devices, on_device(): lax.psum_scatter(combined.reshape(row_tiles * tile_size, block_width), 'r...  229 us
    another operation x27, other arithmetic, upper_cholesky(): return jnp.linalg.cholesky(gram).T  111 us
    all_gather x1, waiting for transfers between devices, on_device(): gathered = lax.all_gather(half_basis, 'col', axis=0, tiled=True)  45.2 us
    ppermute x9, waiting for transfers between devices, swapped(): lax.ppermute(value, axis, [(i, i ^ 1 << bit) for i in range(lax.axis_size...  33.5 us
    ppermute x9, starting transfers between devices, swapped(): lax.ppermute(value, axis, [(i, i ^ 1 << bit) for i in range(lax.axis_size...  28.5 us
  transfers between devices with their start and end apart: 12, of which 12 were waited for; matrix products, arithmetic and copies ran while one was open for 1% of the time, Pallas kernels for 0%

commit v1 on v0

v1 whole, which is shorter than its diff:
```python
import functools

import jax
import jax.numpy as jnp
from jax import lax
from jax.experimental import pallas as pl
from jax.experimental.pallas import tpu as pltpu
from jax.sharding import PartitionSpec as P

HIGHEST = lax.Precision.HIGHEST
MESH = pl.DeviceIdType.MESH
F32 = jnp.float32
BF16 = jnp.bfloat16

NX, NZ, NY, NC = 4, 8, 8, 2
SLOTS = 16
T = 128
AHEAD = (4, 3, 2, 1)
BEHIND = (0, -3, -2, -1)


def dot(a, b, dims):
    return lax.dot_general(a, b, (dims, ((), ())), precision=HIGHEST, preferred_element_type=F32)


def step_kernel(
    rows_ref, cols_ref, count_ref, v_ref, vp_ref, coupling_ref, tiles_ref,
    residual_ref, projection_ref, gram_ref,
    latest, half, gathered, sums, sums16, prev_part, vt,
    fwd, direct, comb, fwd_in, direct_in, comb_in,
    own, zsend, zsend4, zrecv, zrecv4, part,
    red1, red2, red3, piece1, piece2, piece3, totals,
    ring_s, ring_r, pair_s, pair_r, x_s, x_r, z_s, z_r,
    r1_s, r1_r, r2_s, r2_r, r3_s, r3_r, r4_s, r4_r,
):
    row = lax.axis_index("row")
    col = lax.axis_index("col")
    x, z = row // NZ, row % NZ
    y, core = col // NC, col % NC

    def at(dx=0, dz=0, dy=0, dc=0):
        return (
            ((x + dx + NX) % NX) * NZ + (z + dz + NZ) % NZ,
            ((y + dy + NY) % NY) * NC + (core + dc) % NC,
        )

    def copy(src, dst, send, recv, device):
        return pltpu.make_async_remote_copy(
            src_ref=src, dst_ref=dst, send_sem=send, recv_sem=recv, device_id=device, device_id_type=MESH
        )

    barrier = pltpu.get_barrier_semaphore()
    peers = [at(dz=d // 2, dc=d % 2) for d in range(1, 16)]
    peers += [at(dy=d) for d in range(1, NY)] + [at(dx=d) for d in range(1, NX)]
    for peer in peers:
        pl.semaphore_signal(barrier, inc=1, device_id=peer, device_id_type=MESH)

    half[...] = v_ref[...].astype(BF16).reshape(2, T, T)
    pl.semaphore_wait(barrier, len(peers))

    pending = []

    def start(c):
        c.start()
        pending.append(c)
        return c

    def block(origin, h, c):
        return gathered.at[2 * (NC * origin + c) + h]

    def ring(direction, step, h):
        origin = (y - direction * (step - 1) + NY) % NY
        dst = block(origin, h, core)
        src = half.at[h] if step == 1 else dst
        d = 0 if direction == 1 else 1
        return copy(src, dst, ring_s.at[d, step - 1, h], ring_r.at[d, step - 1, h], at(dy=direction))

    def arrived(direction, step, h):
        origin = (y - direction * step + NY) % NY
        d = 0 if direction == 1 else 1
        dst = block(origin, h, core)
        return copy(dst, dst, ring_s.at[d, step - 1, h], ring_r.at[d, step - 1, h], at(dy=direction))

    def to_pair(delta, h):
        origin = (y + delta + NY) % NY
        dst = block(origin, h, core)
        src = half.at[h] if delta == 0 else dst
        k = (delta + NY) % NY
        return copy(src, dst, pair_s.at[k, h], pair_r.at[k, h], at(dc=1))

    def from_pair(delta, h):
        origin = (y + delta + NY) % NY
        dst = block(origin, h, 1 - core)
        k = (delta + NY) % NY
        return copy(dst, dst, pair_s.at[k, h], pair_r.at[k, h], at(dc=1))

    def has(direction, step, h):
        return step < 4 or (step == 4 and (h == 0) == (direction == 1))

    for h in range(2):
        for direction in (1, -1):
            start(ring(direction, 1, h))
    for h in range(2):
        start(to_pair(0, h))

    gathered[pl.ds(2 * col, 2)] = half[...]
    i0 = lax.broadcasted_iota(jnp.int32, (T, T), 0)
    i1 = lax.broadcasted_iota(jnp.int32, (T, T), 1)
    upper = jnp.where(i0 <= i1, coupling_ref[...], 0.0)
    prev_part[...] = dot(vp_ref[...], upper, ((1,), (1,)))
    vt[...] = v_ref[...].T
    sums[SLOTS] = jnp.zeros((T, T), F32)
    sums16[SLOTS] = jnp.zeros((T, T), BF16)
    count = count_ref[0]
    used = [jnp.where(t < count, rows_ref[t], -1) for t in range(SLOTS)]

    def find(r, carry):
        found = jnp.int32(SLOTS)
        for t in range(SLOTS):
            found = jnp.where(used[t] == r, t, found)
        latest[r] = found
        return carry

    lax.fori_loop(0, NX * NZ * 2, find, 0)

    for step in range(1, 5):
        for h in range(2):
            for direction in (1, -1):
                if has(direction, step, h):
                    arrived(direction, step, h).wait_recv()
                    if has(direction, step + 1, h):
                        start(ring(direction, step + 1, h))
                    start(to_pair(-direction * step, h))
    for delta in range(NY):
        for h in range(2):
            from_pair(delta, h).wait_recv()

    for t in range(SLOTS):
        before = jnp.int32(SLOTS)
        for s in range(t):
            before = jnp.where(used[s] == used[t], s, before)
        value = sums[before] + jnp.dot(tiles_ref[t], gathered[cols_ref[t]], preferred_element_type=F32)
        sums[t] = value
        sums16[t] = value.astype(BF16)

    def tile_of(dx, dz, h):
        return 2 * (((x + dx + NX) % NX) * NZ + (z + dz + NZ) % NZ) + h

    def fill(dst, dx, dz):
        for h in range(2):
            dst[h] = sums16[latest[tile_of(dx, dz, h)]]

    def xcopy(kind, s, k):
        src = (fwd, direct, comb)[kind].at[s, k]
        dst = (fwd_in, direct_in, comb_in)[kind].at[s, k]
        return copy(src, dst, x_s.at[kind, s, k], x_r.at[kind, s, k], at(dx=1 if s == 0 else -1))

    side = (AHEAD, BEHIND)

    def send_forward(k):
        for s in range(2):
            fill(fwd.at[s, k], 2, side[s][k])
            start(xcopy(0, s, k))

    def send_direct(k):
        for s in range(2):
            fill(direct.at[s, k], 1 if s == 0 else -1, side[1 - s][k])
            start(xcopy(1, s, k))

    def send_combined(k):
        for s in range(2):
            xcopy(0, s, k).wait_recv()
            for h in range(2):
                mine = sums[latest[tile_of(1 if s == 0 else -1, side[s][k], h)]]
                comb[s, k, h] = (mine + fwd_in[s, k, h].astype(F32)).astype(BF16)
            start(xcopy(2, s, k))

    def zcopy(s, k):
        if k == 0:
            return copy(zsend4.at[s], zrecv4.at[s], z_s.at[s, 0], z_r.at[s, 0], at(dz=1 if s == 0 else -1))
        return copy(zsend.at[s, k - 1], zrecv.at[s, k - 1], z_s.at[s, k], z_r.at[s, k], at(dz=1 if s == 0 else -1))

    def line_sum(s, k, h):
        mine = sums[latest[tile_of(0, side[s][k], h)]]
        return mine + comb_in[s, k, h].astype(F32) + direct_in[1 - s, k, h].astype(F32)

    def finish(k):
        for s in range(2):
            xcopy(2, s, k).wait_recv()
            xcopy(1, 1 - s, k).wait_recv()
            if k == 0:
                if s == 0:
                    for h in range(2):
                        zsend4[h] = line_sum(0, 0, h)
                        start(zcopy(h, 0))
                else:
                    for h in range(2):
                        own[h] = line_sum(1, 0, h)
            else:
                zcopy(s, k - 1).wait_recv()
                for h in range(2):
                    value = line_sum(s, k, h)
                    if k > 1:
                        value = value + zrecv[s, k - 2, h]
                    elif h == s:
                        value = value + zrecv4[s]
                    zsend[s, k - 1, h] = value
                start(zcopy(s, k))

    send_forward(0)
    send_direct(0)
    send_forward(1)
    send_direct(1)
    send_combined(0)
    send_forward(2)
    send_direct(2)
    finish(0)
    send_combined(1)
    send_forward(3)
    send_direct(3)
    finish(1)
    send_combined(2)
    finish(2)
    send_combined(3)
    finish(3)
    for s in range(2):
        zcopy(s, 3).wait_recv()
    product = (own[...] + zrecv[0, 2] + zrecv[1, 2]).reshape(2 * T, T)

    g = z * NC + core

    def group_peer(d):
        h = (g + d) % SLOTS
        return h, (x * NZ + h // NC, y * NC + h % NC)

    def total(n, out_ref):
        for d in range(1, SLOTS):
            h, device = group_peer(d)
            start(copy(part.at[n, pl.ds(8 * h, 8)], red1.at[n, g], r1_s.at[n, d], r1_r.at[n, d], device))
        red1[n, g] = part[n, pl.ds(8 * g, 8)]
        for d in range(1, SLOTS):
            h, device = group_peer(SLOTS - d)
            copy(red1.at[n, h], red1.at[n, h], r1_s.at[n, d], r1_r.at[n, d], device).wait_recv()
        piece1[n] = jnp.sum(red1[n], axis=0)
        for d in range(1, NY):
            start(copy(piece1.at[n], red2.at[n, y], r2_s.at[n, d], r2_r.at[n, d], at(dy=d)))
        red2[n, y] = piece1[n]
        for d in range(1, NY):
            other = (y + NY - d) % NY
            copy(red2.at[n, other], red2.at[n, other], r2_s.at[n, d], r2_r.at[n, d], at(dy=NY - d)).wait_recv()
        piece2[n] = jnp.sum(red2[n], axis=0)
        for d in range(1, NX):
            start(copy(piece2.at[n], red3.at[n, x], r3_s.at[n, d], r3_r.at[n, d], at(dx=d)))
        red3[n, x] = piece2[n]
        for d in range(1, NX):
            other = (x + NX - d) % NX
            copy(red3.at[n, other], red3.at[n, other], r3_s.at[n, d], r3_r.at[n, d], at(dx=NX - d)).wait_recv()
        piece3[n] = jnp.sum(red3[n], axis=0)
        mine = totals.at[n, pl.ds(8 * g, 8)]
        for d in range(1, SLOTS):
            h, device = group_peer(d)
            start(copy(piece3.at[n], mine, r4_s.at[n, d], r4_r.at[n, d], device))
        totals[n, pl.ds(8 * g, 8)] = piece3[n]
        for d in range(1, SLOTS):
            h, device = group_peer(SLOTS - d)
            theirs = totals.at[n, pl.ds(8 * h, 8)]
            copy(theirs, theirs, r4_s.at[n, d], r4_r.at[n, d], device).wait_recv()
        return totals[n]

    scale = float(NX * NZ * NY * NC * 2 * T) ** (-0.5)
    part[0] = dot(vt[...], product, ((1,), (0,)))
    projection = total(0, projection_ref) * scale
    projection_ref[...] = projection
    residual = product - dot(v_ref[...], projection, ((1,), (0,))) * scale - prev_part[...]
    residual_ref[...] = residual
    part[1] = dot(residual, residual, ((0,), (0,)))
    gram_ref[...] = total(1, gram_ref) * (scale * scale)

    for c in pending:
        c.wait_send()


def communicate(rows, cols, count, v, vp, coupling, tiles):
    vmem = pl.BlockSpec(memory_space=pltpu.VMEM)
    smem = pl.BlockSpec(memory_space=pltpu.SMEM)
    dma = pltpu.SemaphoreType.DMA
    pair = (2, 4, 2, T, T)
    return pl.pallas_call(
        step_kernel,
        out_shape=(
            jax.ShapeDtypeStruct((2 * T, T), F32),
            jax.ShapeDtypeStruct((T, T), F32),
            jax.ShapeDtypeStruct((T, T), F32),
        ),
        in_specs=[smem, smem, smem, vmem, vmem, vmem, vmem],
        out_specs=(vmem, vmem, vmem),
        scratch_shapes=[
            pltpu.SMEM((NX * NZ * 2,), jnp.int32),
            pltpu.VMEM((2, T, T), BF16),
            pltpu.VMEM((2 * SLOTS, T, T), BF16),
            pltpu.VMEM((SLOTS + 1, T, T), F32),
            pltpu.VMEM((SLOTS + 1, T, T), BF16),
            pltpu.VMEM((2 * T, T), F32),
            pltpu.VMEM((T, 2 * T), F32),
        ]
        + [pltpu.VMEM(pair, BF16)] * 6
        + [
            pltpu.VMEM((2, T, T), F32),
            pltpu.VMEM((2, 3, 2, T, T), F32),
            pltpu.VMEM((2, T, T), F32),
            pltpu.VMEM((2, 3, 2, T, T), F32),
            pltpu.VMEM((2, T, T), F32),
            pltpu.VMEM((2, T, T), F32),
            pltpu.VMEM((2, SLOTS, 8, T), F32),
            pltpu.VMEM((2, NY, 8, T), F32),
            pltpu.VMEM((2, NX, 8, T), F32),
            pltpu.VMEM((2, 8, T), F32),
            pltpu.VMEM((2, 8, T), F32),
            pltpu.VMEM((2, 8, T), F32),
            pltpu.VMEM((2, T, T), F32),
            dma((2, 4, 2)), dma((2, 4, 2)), dma((NY, 2)), dma((NY, 2)),
            dma((3, 2, 4)), dma((3, 2, 4)), dma((2, 4)), dma((2, 4)),
            dma((2, SLOTS)), dma((2, SLOTS)), dma((2, NY)), dma((2, NY)),
            dma((2, NX)), dma((2, NX)), dma((2, SLOTS)), dma((2, SLOTS)),
        ],
        compiler_params=pltpu.CompilerParams(collective_id=0, has_side_effects=True),
        name="krylov_step",
    )(rows, cols, count, v, vp, coupling, tiles)


def on_device(basis_now, basis_prev, coupling, tiles, tile_rows, tile_cols, tile_counts):
    residual, projection, gram = communicate(
        tile_rows[0, 0], tile_cols[0, 0], tile_counts[0], basis_now, basis_prev, coupling, tiles[0, 0]
    )
    rfactor = jnp.linalg.cholesky(gram).T
    identity = jnp.eye(T, dtype=F32)
    inverse = jax.scipy.linalg.solve_triangular(rfactor.T, identity, lower=True)
    basis = jnp.dot(residual, inverse.T, precision=HIGHEST)
    return (basis, projection, rfactor)


def solution(mesh):
    placed = (
        P(("row", "col"), None),
        P(("row", "col"), None),
        P(),
        P("row", "col", None, None, None),
        P("row", "col", None),
        P("row", "col", None),
        P("row", "col"),
    )
    return jax.shard_map(
        on_device,
        mesh=mesh,
        in_specs=placed,
        out_specs=(P(("row", "col"), None), P(), P()),
        check_vma=False,
    )
```

time: 783 us -> 129 us (0.16)
  the two profiles are of different devices: /device:TPU:2 before, /device:TPU:1 now
where the time goes in v1:
time: 129 us
  Pallas kernels  101 us (78%)
  other arithmetic  22.9 us (18%)
  local copies, waits for them, and re-layouts  2.36 us (2%)
  between operations  1.36 us (1%)
    pallas_call x1, Pallas kernels, communicate(): pl.pallas_call(step_kernel, out_shape=(jax.ShapeDtypeStruct((2 * T, T), F...  101 us
    another operation x3, other arithmetic, on_device(): rfactor = jnp.linalg.cholesky(gram).T  12.4 us
    another operation x1, other arithmetic, on_device(): inverse = jax.scipy.linalg.solve_triangular(rfactor.T, identity, lower=True)  9.81 us

profile of v1, /device:TPU:1, one launch (start us, length us, event | category | flops | bytes accessed | tf_op | source)
XLA Modules:
  0.0 128.5 jit_solution(15604779634338876364)
XLA Ops:
  1.3 100.8 %krylov_step.1 = (f32[256,128]{1,0:T(8,128)}, f32[128,128]{1,0:T(8,128)}, f32[128,128]{1,0:T(8,128)}) custom-call(s32[16]{0:T(128)} %bitcast.19, s32[16]{0:T(128)} %bitcast.20, s32[1]{0:T(128)} %bitcast.17.count_ref, f32[256,128]{1,0:T(8,128)} %v_ref.1, f32[256,128]{1,0:T(8,128)} %vp_ref.1, f32[128,128]{1,0:T(8,128)} %coupling_ref.1, ...), custom_call_target="tpu_custom_call" | custom-call | tf_op jit(solution)/shard_map/krylov_step/pallas_call | solution.py:288
  102.1 0.0 copy-start
  102.1 1.0 copy.10
  103.1 0.0 copy-done
  103.1 11.7 %cholesky.17 = f32[128,128]{1,0:T(8,128)S(1)} custom-call(f32[128,128]{1,0:T(8,128)S(1)} %fusion.2), custom_call_target="Cholesky" | custom-call | tf_op jit(solution)/shard_map/jit(cholesky)/cholesky | solution.py:335
  114.8 0.6 compare_reduce_fusion
  115.5 0.7 fusion.3
  116.1 0.0 copy-start.1
  116.2 0.7 copy.11
  116.9 9.8 %custom-call.7 = f32[1,128,128]{1,2,0:T(8,128)S(1)} custom-call(f32[1,128,128]{2,1,0:T(8,128)S(1)} %get-tuple-element.13), custom_call_target="InvertDiagBlocksLowerTriangular" | custom-call | tf_op jit(solution)/shard_map/jit(_solve_triangular)/triangular_solve | solution.py:337
  126.7 0.2 fusion
  127.0 0.0 copy-done.1
  127.0 0.0 copy-start.2
  127.0 0.9 fusion.4
  127.9 0.0 copy-done.2
  127.9 0.6 copy.14
  (2 shorter events, 0.0 us)
Async XLA Ops:
  102.1 1.0 copy-start
  116.1 10.8 %copy-start.1 = (f32[256,128]{1,0:T(8,128)S(1)}, f32[256,128]{1,0:T(8,128)}, u32[]{:S(2)}) copy-start(f32[256,128]{1,0:T(8,128)} %get-tuple-element.6) | copy-start | bytes 393220
  127.0 0.9 copy-start.2

commit v2 on v1

--- a/solution.py
+++ b/solution.py
@@ -25,8 +25,9 @@
 
 def step_kernel(
     rows_ref, cols_ref, count_ref, v_ref, vp_ref, coupling_ref, tiles_ref,
-    residual_ref, projection_ref, gram_ref,
-    latest, half, gathered, sums, sums16, prev_part, vt,
+    open_ref, late_ref, early_ref,
+    v_s, vp_s, coupling_s, tiles_s, local_sem,
+    latest, before, half, gathered, sums, sums16, prev_part, vt,
     fwd, direct, comb, fwd_in, direct_in, comb_in,
     own, zsend, zsend4, zrecv, zrecv4, part,
     red1, red2, red3, piece1, piece2, piece3, totals,
@@ -55,7 +56,16 @@
     for peer in peers:
         pl.semaphore_signal(barrier, inc=1, device_id=peer, device_id_type=MESH)
 
-    half[...] = v_ref[...].astype(BF16).reshape(2, T, T)
+    loads = [
+        pltpu.make_async_copy(src, dst, local_sem.at[i])
+        for i, (src, dst) in enumerate(
+            ((v_ref, v_s), (vp_ref, vp_s), (coupling_ref, coupling_s), (tiles_ref, tiles_s))
+        )
+    ]
+    for load in loads:
+        load.start()
+    loads[0].wait()
+    half[...] = v_s[...].astype(BF16).reshape(2, T, T)
     pl.semaphore_wait(barrier, len(peers))
 
     pending = []
@@ -103,27 +113,54 @@
     for h in range(2):
         start(to_pair(0, h))
 
-    gathered[pl.ds(2 * col, 2)] = half[...]
-    i0 = lax.broadcasted_iota(jnp.int32, (T, T), 0)
-    i1 = lax.broadcasted_iota(jnp.int32, (T, T), 1)
-    upper = jnp.where(i0 <= i1, coupling_ref[...], 0.0)
-    prev_part[...] = dot(vp_ref[...], upper, ((1,), (1,)))
-    vt[...] = v_ref[...].T
-    sums[SLOTS] = jnp.zeros((T, T), F32)
-    sums16[SLOTS] = jnp.zeros((T, T), BF16)
-    count = count_ref[0]
-    used = [jnp.where(t < count, rows_ref[t], -1) for t in range(SLOTS)]
-
-    def find(r, carry):
-        found = jnp.int32(SLOTS)
-        for t in range(SLOTS):
-            found = jnp.where(used[t] == r, t, found)
-        latest[r] = found
-        return carry
-
-    lax.fori_loop(0, NX * NZ * 2, find, 0)
-
-    for step in range(1, 5):
+    g = z * NC + core
+
+    def group_peer(d):
+        h = (g + d) % SLOTS
+        return h, (x * NZ + h // NC, y * NC + h % NC)
+
+    def scatter(n):
+        for d in range(1, SLOTS):
+            h, device = group_peer(d)
+            start(copy(part.at[n, pl.ds(16 * h, 16)], red1.at[n, g], r1_s.at[n, d], r1_r.at[n, d], device))
+        red1[n, g] = part[n, pl.ds(16 * g, 16)]
+
+    def over_y(n):
+        for d in range(1, SLOTS):
+            h, device = group_peer(SLOTS - d)
+            copy(red1.at[n, h], red1.at[n, h], r1_s.at[n, d], r1_r.at[n, d], device).wait_recv()
+        piece1[n] = jnp.sum(red1[n], axis=0)
+        for d in range(1, NY):
+            start(copy(piece1.at[n], red2.at[n, y], r2_s.at[n, d], r2_r.at[n, d], at(dy=d)))
+        red2[n, y] = piece1[n]
+
+    def over_x(n):
+        for d in range(1, NY):
+            other = (y + NY - d) % NY
+            copy(red2.at[n, other], red2.at[n, other], r2_s.at[n, d], r2_r.at[n, d], at(dy=NY - d)).wait_recv()
+        piece2[n] = jnp.sum(red2[n], axis=0)
+        for d in range(1, NX):
+            start(copy(piece2.at[n], red3.at[n, x], r3_s.at[n, d], r3_r.at[n, d], at(dx=d)))
+        red3[n, x] = piece2[n]
+
+    def back(n):
+        for d in range(1, NX):
+            other = (x + NX - d) % NX
+            copy(red3.at[n, other], red3.at[n, other], r3_s.at[n, d], r3_r.at[n, d], at(dx=NX - d)).wait_recv()
+        piece3[n] = jnp.sum(red3[n], axis=0)
+        mine = totals.at[n, pl.ds(16 * g, 16)]
+        for d in range(1, SLOTS):
+            h, device = group_peer(d)
+            start(copy(piece3.at[n], mine, r4_s.at[n, d], r4_r.at[n, d], device))
+        totals[n, pl.ds(16 * g, 16)] = piece3[n]
+
+    def collect(n):
+        for d in range(1, SLOTS):
+            h, device = group_peer(SLOTS - d)
+            theirs = totals.at[n, pl.ds(16 * h, 16)]
+            copy(theirs, theirs, r4_s.at[n, d], r4_r.at[n, d], device).wait_recv()
+
+    def pass_on(step):
         for h in range(2):
             for direction in (1, -1):
                 if has(direction, step, h):
@@ -131,15 +168,51 @@
                     if has(direction, step + 1, h):
                         start(ring(direction, step + 1, h))
                     start(to_pair(-direction * step, h))
+
+    gathered[pl.ds(2 * col, 2)] = half[...]
+    loads[1].wait()
+    loads[2].wait()
+    i0 = lax.broadcasted_iota(jnp.int32, (T, T), 0)
+    i1 = lax.broadcasted_iota(jnp.int32, (T, T), 1)
+    upper = jnp.where(i0 <= i1, coupling_s[...], 0.0)
+    prev_part[...] = dot(vp_s[...], upper, ((1,), (1,)))
+    vt[...] = v_s[...].T
+    pass_on(1)
+
+    part[1, 0:T] = dot(vt[...], v_s[...], ((1,), (0,)))
+    part[1, T : 2 * T] = dot(vt[...], prev_part[...], ((1,), (0,)))
+    scatter(1)
+    pass_on(2)
+
+    sums[SLOTS] = jnp.zeros((T, T), F32)
+    sums16[SLOTS] = jnp.zeros((T, T), BF16)
+    count = count_ref[0]
+    used = [jnp.where(t < count, rows_ref[t], -1) for t in range(SLOTS)]
+
+    def find(r, carry):
+        found = jnp.int32(SLOTS)
+        for t in range(SLOTS):
+            found = jnp.where(used[t] == r, t, found)
+        latest[r] = found
+        return carry
+
+    lax.fori_loop(0, NX * NZ, find, 0)
+    pass_on(3)
+
+    lax.fori_loop(NX * NZ, NX * NZ * 2, find, 0)
+    for t in range(SLOTS):
+        found = jnp.int32(SLOTS)
+        for s in range(t):
+            found = jnp.where(used[s] == used[t], s, found)
+        before[t] = found
+    loads[3].wait()
+    pass_on(4)
     for delta in range(NY):
         for h in range(2):
             from_pair(delta, h).wait_recv()
 
     for t in range(SLOTS):
-        before = jnp.int32(SLOTS)
-        for s in range(t):
-            before = jnp.where(used[s] == used[t], s, before)
-        value = sums[before] + jnp.dot(tiles_ref[t], gathered[cols_ref[t]], preferred_element_type=F32)
+        value = sums[before[t]] + jnp.dot(tiles_s[t], gathered[cols_ref[t]], preferred_element_type=F32)
         sums[t] = value
         sums16[t] = value.astype(BF16)
 
@@ -211,14 +284,17 @@
     send_direct(0)
     send_forward(1)
     send_direct(1)
+    over_y(1)
     send_combined(0)
     send_forward(2)
     send_direct(2)
     finish(0)
+    over_x(1)
     send_combined(1)
     send_forward(3)
     send_direct(3)
     finish(1)
+    back(1)
     send_combined(2)
     finish(2)
     send_combined(3)
@@ -227,54 +303,18 @@
         zcopy(s, 3).wait_recv()
     product = (own[...] + zrecv[0, 2] + zrecv[1, 2]).reshape(2 * T, T)
 
-    g = z * NC + core
-
-    def group_peer(d):
-        h = (g + d) % SLOTS
-        return h, (x * NZ + h // NC, y * NC + h % NC)
-
-    def total(n, out_ref):
-        for d in range(1, SLOTS):
-            h, device = group_peer(d)
-            start(copy(part.at[n, pl.ds(8 * h, 8)], red1.at[n, g], r1_s.at[n, d], r1_r.at[n, d], device))
-        red1[n, g] = part[n, pl.ds(8 * g, 8)]
-        for d in range(1, SLOTS):
-            h, device = group_peer(SLOTS - d)
-            copy(red1.at[n, h], red1.at[n, h], r1_s.at[n, d], r1_r.at[n, d], device).wait_recv()
-        piece1[n] = jnp.sum(red1[n], axis=0)
-        for d in range(1, NY):
-            start(copy(piece1.at[n], red2.at[n, y], r2_s.at[n, d], r2_r.at[n, d], at(dy=d)))
-        red2[n, y] = piece1[n]
-        for d in range(1, NY):
-            other = (y + NY - d) % NY
-            copy(red2.at[n, other], red2.at[n, other], r2_s.at[n, d], r2_r.at[n, d], at(dy=NY - d)).wait_recv()
-        piece2[n] = jnp.sum(red2[n], axis=0)
-        for d in range(1, NX):
-            start(copy(piece2.at[n], red3.at[n, x], r3_s.at[n, d], r3_r.at[n, d], at(dx=d)))
-        red3[n, x] = piece2[n]
-        for d in range(1, NX):
-            other = (x + NX - d) % NX
-            copy(red3.at[n, other], red3.at[n, other], r3_s.at[n, d], r3_r.at[n, d], at(dx=NX - d)).wait_recv()
-        piece3[n] = jnp.sum(red3[n], axis=0)
-        mine = totals.at[n, pl.ds(8 * g, 8)]
-        for d in range(1, SLOTS):
-            h, device = group_peer(d)
-            start(copy(piece3.at[n], mine, r4_s.at[n, d], r4_r.at[n, d], device))
-        totals[n, pl.ds(8 * g, 8)] = piece3[n]
-        for d in range(1, SLOTS):
-            h, device = group_peer(SLOTS - d)
-            theirs = totals.at[n, pl.ds(8 * h, 8)]
-            copy(theirs, theirs, r4_s.at[n, d], r4_r.at[n, d], device).wait_recv()
-        return totals[n]
-
-    scale = float(NX * NZ * NY * NC * 2 * T) ** (-0.5)
-    part[0] = dot(vt[...], product, ((1,), (0,)))
-    projection = total(0, projection_ref) * scale
-    projection_ref[...] = projection
-    residual = product - dot(v_ref[...], projection, ((1,), (0,))) * scale - prev_part[...]
-    residual_ref[...] = residual
-    part[1] = dot(residual, residual, ((0,), (0,)))
-    gram_ref[...] = total(1, gram_ref) * (scale * scale)
+    opened = product - prev_part[...]
+    part[0, 0:T] = dot(vt[...], product, ((1,), (0,)))
+    part[0, T : 2 * T] = dot(opened, opened, ((0,), (0,)))
+    scatter(0)
+    open_ref[...] = opened
+    collect(1)
+    early_ref[...] = totals[1]
+    over_y(0)
+    over_x(0)
+    back(0)
+    collect(0)
+    late_ref[...] = totals[0]
 
     for c in pending:
         c.wait_send()
@@ -289,13 +329,19 @@
         step_kernel,
         out_shape=(
             jax.ShapeDtypeStruct((2 * T, T), F32),
-            jax.ShapeDtypeStruct((T, T), F32),
-            jax.ShapeDtypeStruct((T, T), F32),
+            jax.ShapeDtypeStruct((2 * T, T), F32),
+            jax.ShapeDtypeStruct((2 * T, T), F32),
         ),
-        in_specs=[smem, smem, smem, vmem, vmem, vmem, vmem],
+        in_specs=[smem, smem, smem] + [pl.BlockSpec(memory_space=pl.ANY)] * 4,
         out_specs=(vmem, vmem, vmem),
         scratch_shapes=[
+            pltpu.VMEM((2 * T, T), F32),
+            pltpu.VMEM((2 * T, T), F32),
+            pltpu.VMEM((T, T), F32),
+            pltpu.VMEM((SLOTS, T, T), BF16),
+            dma((4,)),
             pltpu.SMEM((NX * NZ * 2,), jnp.int32),
+            pltpu.SMEM((SLOTS,), jnp.int32),
             pltpu.VMEM((2, T, T), BF16),
             pltpu.VMEM((2 * SLOTS, T, T), BF16),
             pltpu.VMEM((SLOTS + 1, T, T), F32),
@@ -310,14 +356,14 @@
             pltpu.VMEM((2, T, T), F32),
             pltpu.VMEM((2, 3, 2, T, T), F32),
             pltpu.VMEM((2, T, T), F32),
-            pltpu.VMEM((2, T, T), F32),
-            pltpu.VMEM((2, SLOTS, 8, T), F32),
-            pltpu.VMEM((2, NY, 8, T), F32),
-            pltpu.VMEM((2, NX, 8, T), F32),
-            pltpu.VMEM((2, 8, T), F32),
-            pltpu.VMEM((2, 8, T), F32),
-            pltpu.VMEM((2, 8, T), F32),
-            pltpu.VMEM((2, T, T), F32),
+            pltpu.VMEM((2, 2 * T, T), F32),
+            pltpu.VMEM((2, SLOTS, 16, T), F32),
+            pltpu.VMEM((2, NY, 16, T), F32),
+            pltpu.VMEM((2, NX, 16, T), F32),
+            pltpu.VMEM((2, 16, T), F32),
+            pltpu.VMEM((2, 16, T), F32),
+            pltpu.VMEM((2, 16, T), F32),
+            pltpu.VMEM((2, 2 * T, T), F32),
             dma((2, 4, 2)), dma((2, 4, 2)), dma((NY, 2)), dma((NY, 2)),
             dma((3, 2, 4)), dma((3, 2, 4)), dma((2, 4)), dma((2, 4)),
             dma((2, SLOTS)), dma((2, SLOTS)), dma((2, NY)), dma((2, NY)),
@@ -328,15 +374,91 @@
     )(rows, cols, count, v, vp, coupling, tiles)
 
 
+def factor_kernel(total, late_ref, early_ref, open_ref, v_ref, basis_ref, projection_ref, rfactor_ref, residual, inverse_ref):
+    image = late_ref[0:T]
+    along = image * (1.0 / total)
+    projection_ref[...] = image * total ** (-0.5)
+    residual[...] = open_ref[...] - dot(v_ref[...], along, ((1,), (0,)))
+    inner = (image - early_ref[T : 2 * T]) * (1.0 / total)
+    inner = inner - 0.5 * dot(early_ref[0:T] * (1.0 / total), along, ((1,), (0,)))
+    cross = dot(along, inner, ((0,), (0,)))
+    gram = late_ref[T : 2 * T] * (1.0 / total) - cross - cross.T
+    lane = lax.broadcasted_iota(jnp.int32, (1, T), 1)
+    groups = T // 8
+    left = [gram[8 * i : 8 * i + 8] for i in range(groups)]
+    sub8 = lax.broadcasted_iota(jnp.int32, (8, T), 0)
+    lane8 = lax.broadcasted_iota(jnp.int32, (8, T), 1)
+    right = [jnp.where(lane8 == sub8 + 8 * i, 1.0, 0.0).astype(F32) for i in range(groups)]
+
+    def spread(row):
+        return jnp.broadcast_to(row, (8, T))
+
+    for p in range(groups):
+        panel, other = left[p], right[p]
+        columns = [jnp.broadcast_to(panel[:, 8 * p + j : 8 * p + j + 1], (8, T)) for j in range(8)]
+        a = [[spread(columns[j][i : i + 1]) for j in range(i + 1)] for i in range(8)]
+        inv = [[None] * 8 for _ in range(8)]
+        low = [[None] * 8 for _ in range(8)]
+        for j in range(8):
+            inv[j][j] = lax.rsqrt(a[j][j])
+            for i in range(j + 1, 8):
+                low[i][j] = a[i][j] * inv[j][j]
+            for i in range(j + 1, 8):
+                for k in range(j + 1, i + 1):
+                    a[i][k] = a[i][k] - low[i][j] * low[k][j]
+            for k in range(j):
+                s = low[j][k] * inv[k][k]
+                for m in range(k + 1, j):
+                    s = s + low[j][m] * inv[m][k]
+                inv[j][k] = -(s * inv[j][j])
+        rows_l = [spread(panel[j : j + 1]) for j in range(8)]
+        rows_r = [spread(other[j : j + 1]) for j in range(8)]
+
+        def mix(rows, weight, picks):
+            value = None
+            for j in picks:
+                term = weight(j) * rows[j]
+                value = term if value is None else value + term
+            return value
+
+        out_l = [mix(rows_l, lambda j, i=i: inv[i][j], range(i + 1)) for i in range(8)]
+        out_r = [mix(rows_r, lambda j, i=i: inv[i][j], range(i + 1)) for i in range(8)]
+        for i in range(8):
+            r = 8 * p + i
+            rfactor_ref[pl.ds(r, 1)] = jnp.where(lane >= r, out_l[i][0:1], 0.0)
+            inverse_ref[pl.ds(r, 1)] = out_r[i][0:1]
+        if p + 1 < groups:
+            back_l = [mix(out_l, lambda i, j=j: inv[i][j], range(j, 8)) for j in range(8)]
+            back_r = [mix(out_r, lambda i, j=j: inv[i][j], range(j, 8)) for j in range(8)]
+            for g in range(p + 1, groups):
+                cols = [jnp.broadcast_to(left[g][:, 8 * p + j : 8 * p + j + 1], (8, T)) for j in range(8)]
+                left[g] = left[g] - mix(back_l, lambda j: cols[j], range(8))
+                right[g] = right[g] - mix(back_r, lambda j: cols[j], range(8))
+    basis_ref[...] = dot(residual[...], inverse_ref[...], ((1,), (1,)))
+
+
+def factor(total, late, early, opened, v):
+    vmem = pl.BlockSpec(memory_space=pltpu.VMEM)
+    return pl.pallas_call(
+        functools.partial(factor_kernel, total),
+        out_shape=(
+            jax.ShapeDtypeStruct((2 * T, T), F32),
+            jax.ShapeDtypeStruct((T, T), F32),
+            jax.ShapeDtypeStruct((T, T), F32),
+        ),
+        in_specs=[vmem] * 4,
+        out_specs=(vmem,) * 3,
+        scratch_shapes=[pltpu.VMEM((2 * T, T), F32), pltpu.VMEM((T, T), F32)],
+        name="factor",
+    )(late, early, opened, v)
+
+
 def on_device(basis_now, basis_prev, coupling, tiles, tile_rows, tile_cols, tile_counts):
-    residual, projection, gram = communicate(
+    opened, late, early = communicate(
         tile_rows[0, 0], tile_cols[0, 0], tile_counts[0], basis_now, basis_prev, coupling, tiles[0, 0]
     )
-    rfactor = jnp.linalg.cholesky(gram).T
-    identity = jnp.eye(T, dtype=F32)
-    inverse = jax.scipy.linalg.solve_triangular(rfactor.T, identity, lower=True)
-    basis = jnp.dot(residual, inverse.T, precision=HIGHEST)
-    return (basis, projection, rfactor)
+    total = float(NX * NZ * NY * NC * 2 * T)
+    return factor(total, late, early, opened, basis_now)
 
 
 def solution(mesh):

time: 129 us -> 93.5 us (0.72)
  other arithmetic: 22.9 us -> 0 us
  Pallas kernels: 101 us -> 92 us
  local copies, waits for them, and re-layouts: 2.36 us -> 0 us
    another operation x4 -> x0, other arithmetic: 22.2 us -> none  [the longest x3 12.4 us: on_device(): rfactor = jnp.linalg.cholesky(gram).T]
    pallas_call x1, Pallas kernels: 101 us -> 84 us  [communicate(): pl.pallas_call(step_kernel, out_shape=(jax.ShapeDtypeStruct((2 * T, T), F...]
    pallas_call x0 -> x1, Pallas kernels: none -> 7.99 us  [factor(): pl.pallas_call(functools.partial(factor_kernel, total), out_shape=(jax.Sh...]
    unnamed x8 -> x0, local copies, waits for them, and re-layouts: 1.37 us -> none
where the time goes in v2:
time: 93.5 us; the launch traced here: 93.3 us
  Pallas kernels  92 us (98%)
  between operations  1.29 us (1%)
    pallas_call x1, Pallas kernels, communicate(): pl.pallas_call(step_kernel, out_shape=(jax.ShapeDtypeStruct((2 * T, T), F...  84 us
    pallas_call x1, Pallas kernels, factor(): pl.pallas_call(functools.partial(factor_kernel, total), out_shape=(jax.Sh...  7.99 us

profile of v2, /device:TPU:1, one launch (start us, length us, event | category | flops | bytes accessed | tf_op | source)
XLA Modules:
  0.0 93.3 jit_solution(5497601617490108132)
XLA Ops:
  1.3 84.0 %krylov_step.1 = (f32[256,128]{1,0:T(8,128)}, f32[256,128]{1,0:T(8,128)}, f32[256,128]{1,0:T(8,128)}) custom-call(s32[16]{0:T(128)} %bitcast.6, s32[16]{0:T(128)} %bitcast.7, s32[1]{0:T(128)} %bitcast.4.count_ref, f32[256,128]{1,0:T(8,128)} %v_ref.3, f32[256,128]{1,0:T(8,128)} %vp_ref.1, f32[128,128]{1,0:T(8,128)} %coupling_ref.1, bf16[16,128,128]{2,1,0:T(8,128)(2,1)} %bitcast.5), custom_call_target="tpu_custom_call" | custom-call | tf_op jit(solution)/shard_map/krylov_step/pallas_call | solution.py:328
  85.3 8.0 %factor.1 = (f32[256,128]{1,0:T(8,128)}, f32[128,128]{1,0:T(8,128)}, f32[128,128]{1,0:T(8,128)}) custom-call(f32[256,128]{1,0:T(8,128)} %get-tuple-element.6.late_ref, f32[256,128]{1,0:T(8,128)} %get-tuple-element.7.early_ref, f32[256,128]{1,0:T(8,128)} %get-tuple-element.8.open_ref, f32[256,128]{1,0:T(8,128)} %v_ref.3), custom_call_target="tpu_custom_call" | custom-call | tf_op jit(solution)/shard_map/factor/pallas_call | solution.py:442

commit v3 on v2

--- a/solution.py
+++ b/solution.py
@@ -16,7 +16,7 @@
 SLOTS = 16
 T = 128
 AHEAD = (4, 3, 2, 1)
-BEHIND = (0, -3, -2, -1)
+BEHIND = (-3, -2, -1, 0)
 
 
 def dot(a, b, dims):
@@ -29,7 +29,7 @@
     v_s, vp_s, coupling_s, tiles_s, local_sem,
     latest, before, half, gathered, sums, sums16, prev_part, vt,
     fwd, direct, comb, fwd_in, direct_in, comb_in,
-    own, zsend, zsend4, zrecv, zrecv4, part,
+    own, zsend, zrecv, part,
     red1, red2, red3, piece1, piece2, piece3, totals,
     ring_s, ring_r, pair_s, pair_r, x_s, x_r, z_s, z_r,
     r1_s, r1_r, r2_s, r2_r, r3_s, r3_r, r4_s, r4_r,
@@ -78,18 +78,19 @@
     def block(origin, h, c):
         return gathered.at[2 * (NC * origin + c) + h]
 
-    def ring(direction, step, h):
-        origin = (y - direction * (step - 1) + NY) % NY
-        dst = block(origin, h, core)
-        src = half.at[h] if step == 1 else dst
+    def along(direction, far, h):
         d = 0 if direction == 1 else 1
-        return copy(src, dst, ring_s.at[d, step - 1, h], ring_r.at[d, step - 1, h], at(dy=direction))
-
-    def arrived(direction, step, h):
-        origin = (y - direction * step + NY) % NY
+        if far <= 2:
+            src, dst, device = half.at[h], block(y, h, core), at(dy=far * direction)
+        else:
+            dst = block((y - 2 * direction + NY) % NY, h, core)
+            src, device = dst, at(dy=(far - 2) * direction)
+        return copy(src, dst, ring_s.at[d, far - 1, h], ring_r.at[d, far - 1, h], device)
+
+    def arrived(direction, far, h):
         d = 0 if direction == 1 else 1
-        dst = block(origin, h, core)
-        return copy(dst, dst, ring_s.at[d, step - 1, h], ring_r.at[d, step - 1, h], at(dy=direction))
+        dst = block((y - direction * far + NY) % NY, h, core)
+        return copy(dst, dst, ring_s.at[d, far - 1, h], ring_r.at[d, far - 1, h], at(dy=direction))
 
     def to_pair(delta, h):
         origin = (y + delta + NY) % NY
@@ -104,12 +105,13 @@
         k = (delta + NY) % NY
         return copy(dst, dst, pair_s.at[k, h], pair_r.at[k, h], at(dc=1))
 
-    def has(direction, step, h):
-        return step < 4 or (step == 4 and (h == 0) == (direction == 1))
-
-    for h in range(2):
-        for direction in (1, -1):
-            start(ring(direction, 1, h))
+    def has(direction, far, h):
+        return far < 4 or (h == 0) == (direction == 1)
+
+    for far in (2, 1):
+        for h in range(2):
+            for direction in (1, -1):
+                start(along(direction, far, h))
     for h in range(2):
         start(to_pair(0, h))
 
@@ -160,14 +162,16 @@
             theirs = totals.at[n, pl.ds(16 * h, 16)]
             copy(theirs, theirs, r4_s.at[n, d], r4_r.at[n, d], device).wait_recv()
 
-    def pass_on(step):
+    def take(far):
         for h in range(2):
             for direction in (1, -1):
-                if has(direction, step, h):
-                    arrived(direction, step, h).wait_recv()
-                    if has(direction, step + 1, h):
-                        start(ring(direction, step + 1, h))
-                    start(to_pair(-direction * step, h))
+                if has(direction, far, h):
+                    arrived(direction, far, h).wait_recv()
+                    if far == 2:
+                        start(along(direction, 3, h))
+                        if has(direction, 4, h):
+                            start(along(direction, 4, h))
+                    start(to_pair(-direction * far, h))
 
     gathered[pl.ds(2 * col, 2)] = half[...]
     loads[1].wait()
@@ -177,12 +181,12 @@
     upper = jnp.where(i0 <= i1, coupling_s[...], 0.0)
     prev_part[...] = dot(vp_s[...], upper, ((1,), (1,)))
     vt[...] = v_s[...].T
-    pass_on(1)
+    take(2)
 
     part[1, 0:T] = dot(vt[...], v_s[...], ((1,), (0,)))
     part[1, T : 2 * T] = dot(vt[...], prev_part[...], ((1,), (0,)))
     scatter(1)
-    pass_on(2)
+    take(1)
 
     sums[SLOTS] = jnp.zeros((T, T), F32)
     sums16[SLOTS] = jnp.zeros((T, T), BF16)
@@ -196,17 +200,15 @@
         latest[r] = found
         return carry
 
-    lax.fori_loop(0, NX * NZ, find, 0)
-    pass_on(3)
-
-    lax.fori_loop(NX * NZ, NX * NZ * 2, find, 0)
+    lax.fori_loop(0, NX * NZ * 2, find, 0)
     for t in range(SLOTS):
         found = jnp.int32(SLOTS)
         for s in range(t):
             found = jnp.where(used[s] == used[t], s, found)
         before[t] = found
     loads[3].wait()
-    pass_on(4)
+    take(3)
+    take(4)
     for delta in range(NY):
         for h in range(2):
             from_pair(delta, h).wait_recv()
@@ -249,9 +251,7 @@
             start(xcopy(2, s, k))
 
     def zcopy(s, k):
-        if k == 0:
-            return copy(zsend4.at[s], zrecv4.at[s], z_s.at[s, 0], z_r.at[s, 0], at(dz=1 if s == 0 else -1))
-        return copy(zsend.at[s, k - 1], zrecv.at[s, k - 1], z_s.at[s, k], z_r.at[s, k], at(dz=1 if s == 0 else -1))
+        return copy(zsend.at[s, k], zrecv.at[s, k], z_s.at[s, k], z_r.at[s, k], at(dz=side[s][k]))
 
     def line_sum(s, k, h):
         mine = sums[latest[tile_of(0, side[s][k], h)]]
@@ -261,23 +261,12 @@
         for s in range(2):
             xcopy(2, s, k).wait_recv()
             xcopy(1, 1 - s, k).wait_recv()
-            if k == 0:
-                if s == 0:
-                    for h in range(2):
-                        zsend4[h] = line_sum(0, 0, h)
-                        start(zcopy(h, 0))
+            for h in range(2):
+                if side[s][k] == 0:
+                    own[h] = line_sum(s, k, h)
                 else:
-                    for h in range(2):
-                        own[h] = line_sum(1, 0, h)
-            else:
-                zcopy(s, k - 1).wait_recv()
-                for h in range(2):
-                    value = line_sum(s, k, h)
-                    if k > 1:
-                        value = value + zrecv[s, k - 2, h]
-                    elif h == s:
-                        value = value + zrecv4[s]
-                    zsend[s, k - 1, h] = value
+                    zsend[s, k, h] = line_sum(s, k, h).astype(BF16)
+            if side[s][k] != 0:
                 start(zcopy(s, k))
 
     send_forward(0)
@@ -288,20 +277,24 @@
     send_combined(0)
     send_forward(2)
     send_direct(2)
-    finish(0)
-    over_x(1)
     send_combined(1)
     send_forward(3)
     send_direct(3)
+    finish(0)
+    over_x(1)
+    send_combined(2)
     finish(1)
+    send_combined(3)
     back(1)
-    send_combined(2)
     finish(2)
-    send_combined(3)
     finish(3)
-    for s in range(2):
-        zcopy(s, 3).wait_recv()
-    product = (own[...] + zrecv[0, 2] + zrecv[1, 2]).reshape(2 * T, T)
+    product = own[...]
+    for k in range(4):
+        for s in range(2):
+            if side[s][k] != 0:
+                zcopy(s, k).wait_recv()
+                product = product + zrecv[s, k].astype(F32)
+    product = product.reshape(2 * T, T)
 
     opened = product - prev_part[...]
     part[0, 0:T] = dot(vt[...], product, ((1,), (0,)))
@@ -352,10 +345,8 @@
         + [pltpu.VMEM(pair, BF16)] * 6
         + [
             pltpu.VMEM((2, T, T), F32),
-            pltpu.VMEM((2, 3, 2, T, T), F32),
-            pltpu.VMEM((2, T, T), F32),
-            pltpu.VMEM((2, 3, 2, T, T), F32),
-            pltpu.VMEM((2, T, T), F32),
+            pltpu.VMEM(pair, BF16),
+            pltpu.VMEM(pair, BF16),
             pltpu.VMEM((2, 2 * T, T), F32),
             pltpu.VMEM((2, SLOTS, 16, T), F32),
             pltpu.VMEM((2, NY, 16, T), F32),

time: 93.5 us -> 88.5 us (0.947)
  Pallas kernels: 92 us -> 87 us
    pallas_call x1, Pallas kernels: 84 us -> 79 us  [communicate(): pl.pallas_call(step_kernel, out_shape=(jax.ShapeDtypeStruct((2 * T, T), F...]
where the time goes in v3:
time: 88.5 us; the launch traced here: 88.3 us
  Pallas kernels  87 us (98%)
  between operations  1.29 us (1%)
    pallas_call x1, Pallas kernels, communicate(): pl.pallas_call(step_kernel, out_shape=(jax.ShapeDtypeStruct((2 * T, T), F...  79 us
    pallas_call x1, Pallas kernels, factor(): pl.pallas_call(functools.partial(factor_kernel, total), out_shape=(jax.Sh...  7.99 us

profile of v3, /device:TPU:1, one launch (start us, length us, event | category | flops | bytes accessed | tf_op | source)
XLA Modules:
  0.0 88.3 jit_solution(16935332929560081801)
XLA Ops:
  1.3 79.0 %krylov_step.1 = (f32[256,128]{1,0:T(8,128)}, f32[256,128]{1,0:T(8,128)}, f32[256,128]{1,0:T(8,128)}) custom-call(s32[16]{0:T(128)} %bitcast.6, s32[16]{0:T(128)} %bitcast.7, s32[1]{0:T(128)} %bitcast.4.count_ref, f32[256,128]{1,0:T(8,128)} %v_ref.3, f32[256,128]{1,0:T(8,128)} %vp_ref.1, f32[128,128]{1,0:T(8,128)} %coupling_ref.1, bf16[16,128,128]{2,1,0:T(8,128)(2,1)} %bitcast.5), custom_call_target="tpu_custom_call" | custom-call | tf_op jit(solution)/shard_map/krylov_step/pallas_call | solution.py:321
  80.3 8.0 %factor.1 = (f32[256,128]{1,0:T(8,128)}, f32[128,128]{1,0:T(8,128)}, f32[128,128]{1,0:T(8,128)}) custom-call(f32[256,128]{1,0:T(8,128)} %get-tuple-element.6.late_ref, f32[256,128]{1,0:T(8,128)} %get-tuple-element.7.early_ref, f32[256,128]{1,0:T(8,128)} %get-tuple-element.8.open_ref, f32[256,128]{1,0:T(8,128)} %v_ref.3), custom_call_target="tpu_custom_call" | custom-call | tf_op jit(solution)/shard_map/factor/pallas_call | solution.py:433

commit v4 on v3

--- a/solution.py
+++ b/solution.py
@@ -16,7 +16,7 @@
 SLOTS = 16
 T = 128
 AHEAD = (4, 3, 2, 1)
-BEHIND = (-3, -2, -1, 0)
+BEHIND = (0, -3, -2, -1)
 
 
 def dot(a, b, dims):
@@ -29,10 +29,9 @@
     v_s, vp_s, coupling_s, tiles_s, local_sem,
     latest, before, half, gathered, sums, sums16, prev_part, vt,
     fwd, direct, comb, fwd_in, direct_in, comb_in,
-    own, zsend, zrecv, part,
-    red1, red2, red3, piece1, piece2, piece3, totals,
-    ring_s, ring_r, pair_s, pair_r, x_s, x_r, z_s, z_r,
-    r1_s, r1_r, r2_s, r2_r, r3_s, r3_r, r4_s, r4_r,
+    own, zsend, zrecv, zhalf, zhalf_in,
+    ring_s, ring_r, pair_s, pair_r, x_s, x_r, z_s, z_r, zh_s, zh_r,
+    *sum_refs,
 ):
     row = lax.axis_index("row")
     col = lax.axis_index("col")
@@ -52,7 +51,7 @@
 
     barrier = pltpu.get_barrier_semaphore()
     peers = [at(dz=d // 2, dc=d % 2) for d in range(1, 16)]
-    peers += [at(dy=d) for d in range(1, NY)] + [at(dx=d) for d in range(1, NX)]
+    peers += [at(dy=d) for d in range(1, NY)] + [at(dx=d, dc=c) for d in range(1, NX) for c in range(2)]
     for peer in peers:
         pl.semaphore_signal(barrier, inc=1, device_id=peer, device_id_type=MESH)
 
@@ -115,52 +114,69 @@
     for h in range(2):
         start(to_pair(0, h))
 
-    g = z * NC + core
-
-    def group_peer(d):
-        h = (g + d) % SLOTS
-        return h, (x * NZ + h // NC, y * NC + h % NC)
-
-    def scatter(n):
-        for d in range(1, SLOTS):
-            h, device = group_peer(d)
-            start(copy(part.at[n, pl.ds(16 * h, 16)], red1.at[n, g], r1_s.at[n, d], r1_r.at[n, d], device))
-        red1[n, g] = part[n, pl.ds(16 * g, 16)]
-
-    def over_y(n):
-        for d in range(1, SLOTS):
-            h, device = group_peer(SLOTS - d)
-            copy(red1.at[n, h], red1.at[n, h], r1_s.at[n, d], r1_r.at[n, d], device).wait_recv()
-        piece1[n] = jnp.sum(red1[n], axis=0)
-        for d in range(1, NY):
-            start(copy(piece1.at[n], red2.at[n, y], r2_s.at[n, d], r2_r.at[n, d], at(dy=d)))
-        red2[n, y] = piece1[n]
-
-    def over_x(n):
-        for d in range(1, NY):
-            other = (y + NY - d) % NY
-            copy(red2.at[n, other], red2.at[n, other], r2_s.at[n, d], r2_r.at[n, d], at(dy=NY - d)).wait_recv()
-        piece2[n] = jnp.sum(red2[n], axis=0)
-        for d in range(1, NX):
-            start(copy(piece2.at[n], red3.at[n, x], r3_s.at[n, d], r3_r.at[n, d], at(dx=d)))
-        red3[n, x] = piece2[n]
-
-    def back(n):
-        for d in range(1, NX):
-            other = (x + NX - d) % NX
-            copy(red3.at[n, other], red3.at[n, other], r3_s.at[n, d], r3_r.at[n, d], at(dx=NX - d)).wait_recv()
-        piece3[n] = jnp.sum(red3[n], axis=0)
-        mine = totals.at[n, pl.ds(16 * g, 16)]
-        for d in range(1, SLOTS):
-            h, device = group_peer(d)
-            start(copy(piece3.at[n], mine, r4_s.at[n, d], r4_r.at[n, d], device))
-        totals[n, pl.ds(16 * g, 16)] = piece3[n]
-
-    def collect(n):
-        for d in range(1, SLOTS):
-            h, device = group_peer(SLOTS - d)
-            theirs = totals.at[n, pl.ds(16 * h, 16)]
-            copy(theirs, theirs, r4_s.at[n, d], r4_r.at[n, d], device).wait_recv()
+    class Sum:
+        def __init__(self, refs, over_z):
+            self.part, self.totals, self.red, self.piece, self.send, self.recv = (
+                refs[0], refs[1], refs[2:5], refs[5:8], refs[8:12], refs[12:16]
+            )
+            self.over_z = over_z
+            self.place = (z if over_z else x) * NC + core
+            self.last = x if over_z else z
+            self.group, self.size, _ = self.red[0].shape
+
+        def member(self, d):
+            h = (self.place + d) % self.group
+            if self.over_z:
+                return h, (x * NZ + h // NC, y * NC + h % NC)
+            return h, ((h // NC) * NZ + z, y * NC + h % NC)
+
+        def rows(self, ref, h):
+            return ref.at[pl.ds(self.size * h, self.size)]
+
+        def move(self, stage, d, src, dst, device):
+            return copy(src, dst, self.send[stage].at[d], self.recv[stage].at[d], device)
+
+        def scatter(self):
+            for d in range(1, self.group):
+                h, device = self.member(d)
+                start(self.move(0, d, self.rows(self.part, h), self.red[0].at[self.place], device))
+            self.red[0][self.place] = self.part[pl.ds(self.size * self.place, self.size)]
+
+        def reduce(self, stage, i):
+            red, piece = self.red[stage], self.piece[stage]
+            n = red.shape[0]
+            for d in range(1, n):
+                slot = red.at[(i + n - d) % n]
+                self.move(stage, d, slot, slot, at(dc=1)).wait_recv()
+            piece[...] = jnp.sum(red[...], axis=0)
+            return piece
+
+        def spread(self, stage, piece, i, device_at):
+            red = self.red[stage]
+            for d in range(1, red.shape[0]):
+                start(self.move(stage, d, piece, red.at[i], device_at(d)))
+            red[i] = piece[...]
+
+        def over_y(self):
+            self.spread(1, self.reduce(0, self.place), y, lambda d: at(dy=d))
+
+        def over_last(self):
+            piece = self.reduce(1, y)
+            self.spread(2, piece, self.last, (lambda d: at(dx=d)) if self.over_z else (lambda d: at(dz=d)))
+
+        def back(self):
+            piece = self.reduce(2, self.last)
+            for d in range(1, self.group):
+                h, device = self.member(d)
+                start(self.move(3, d, piece, self.rows(self.totals, self.place), device))
+            self.totals[pl.ds(self.size * self.place, self.size)] = piece[...]
+
+        def collect(self):
+            for d in range(1, self.group):
+                slot = self.rows(self.totals, (self.place + self.group - d) % self.group)
+                self.move(3, d, slot, slot, at(dc=1)).wait_recv()
+
+    image, square, early = (Sum(sum_refs[16 * i : 16 * i + 16], over_z) for i, over_z in enumerate((True, False, True)))
 
     def take(far):
         for h in range(2):
@@ -181,11 +197,10 @@
     upper = jnp.where(i0 <= i1, coupling_s[...], 0.0)
     prev_part[...] = dot(vp_s[...], upper, ((1,), (1,)))
     vt[...] = v_s[...].T
+    early.part[0:T] = dot(vt[...], v_s[...], ((1,), (0,)))
+    early.part[T : 2 * T] = dot(vt[...], prev_part[...], ((1,), (0,)))
+    early.scatter()
     take(2)
-
-    part[1, 0:T] = dot(vt[...], v_s[...], ((1,), (0,)))
-    part[1, T : 2 * T] = dot(vt[...], prev_part[...], ((1,), (0,)))
-    scatter(1)
     take(1)
 
     sums[SLOTS] = jnp.zeros((T, T), F32)
@@ -207,6 +222,7 @@
             found = jnp.where(used[s] == used[t], s, found)
         before[t] = found
     loads[3].wait()
+    early.over_y()
     take(3)
     take(4)
     for delta in range(NY):
@@ -253,6 +269,9 @@
     def zcopy(s, k):
         return copy(zsend.at[s, k], zrecv.at[s, k], z_s.at[s, k], z_r.at[s, k], at(dz=side[s][k]))
 
+    def zhalf_copy(s):
+        return copy(zhalf.at[s], zhalf_in.at[s], zh_s.at[s], zh_r.at[s], at(dz=1 if s == 0 else -1))
+
     def line_sum(s, k, h):
         mine = sums[latest[tile_of(0, side[s][k], h)]]
         return mine + comb_in[s, k, h].astype(F32) + direct_in[1 - s, k, h].astype(F32)
@@ -261,56 +280,80 @@
         for s in range(2):
             xcopy(2, s, k).wait_recv()
             xcopy(1, 1 - s, k).wait_recv()
+            if k == 1:
+                zhalf_copy(s).wait_recv()
             for h in range(2):
-                if side[s][k] == 0:
-                    own[h] = line_sum(s, k, h)
+                value = line_sum(s, k, h)
+                if k == 0 and s == 0:
+                    zhalf[h] = value.astype(BF16)
+                    start(zhalf_copy(h))
+                elif k == 0:
+                    own[h] = value
                 else:
-                    zsend[s, k, h] = line_sum(s, k, h).astype(BF16)
-            if side[s][k] != 0:
+                    if k == 1 and h == s:
+                        value = value + zhalf_in[s].astype(F32)
+                    zsend[s, k, h] = value.astype(BF16)
+            if k > 0:
                 start(zcopy(s, k))
 
     send_forward(0)
+    send_forward(1)
     send_direct(0)
-    send_forward(1)
+    send_forward(2)
+    early.over_last()
+    send_combined(0)
     send_direct(1)
-    over_y(1)
-    send_combined(0)
-    send_forward(2)
+    send_forward(3)
+    send_combined(1)
+    early.back()
     send_direct(2)
-    send_combined(1)
-    send_forward(3)
+    finish(0)
+    send_combined(2)
     send_direct(3)
-    finish(0)
-    over_x(1)
-    send_combined(2)
     finish(1)
     send_combined(3)
-    back(1)
     finish(2)
     finish(3)
     product = own[...]
-    for k in range(4):
+    for k in range(1, 4):
         for s in range(2):
-            if side[s][k] != 0:
-                zcopy(s, k).wait_recv()
-                product = product + zrecv[s, k].astype(F32)
+            zcopy(s, k).wait_recv()
+            product = product + zrecv[s, k].astype(F32)
     product = product.reshape(2 * T, T)
 
     opened = product - prev_part[...]
-    part[0, 0:T] = dot(vt[...], product, ((1,), (0,)))
-    part[0, T : 2 * T] = dot(opened, opened, ((0,), (0,)))
-    scatter(0)
+    image.part[...] = dot(vt[...], product, ((1,), (0,)))
+    image.scatter()
+    square.part[...] = dot(opened, opened, ((0,), (0,)))
+    square.scatter()
     open_ref[...] = opened
-    collect(1)
-    early_ref[...] = totals[1]
-    over_y(0)
-    over_x(0)
-    back(0)
-    collect(0)
-    late_ref[...] = totals[0]
+    early.collect()
+    early_ref[...] = early.totals[...]
+    square.over_y()
+    image.over_y()
+    square.over_last()
+    image.over_last()
+    image.back()
+    square.back()
+    image.collect()
+    square.collect()
+    late_ref[0:T] = image.totals[...]
+    late_ref[T : 2 * T] = square.totals[...]
 
     for c in pending:
         c.wait_send()
+
+
+def sum_scratch(rows, group, last):
+    size = rows // group
+    counts = (group, NY, last)
+    sems = [pltpu.SemaphoreType.DMA((n,)) for n in counts + (group,)]
+    return (
+        [pltpu.VMEM((rows, T), F32)] * 2
+        + [pltpu.VMEM((n, size, T), F32) for n in counts]
+        + [pltpu.VMEM((size, T), F32)] * 3
+        + sems * 2
+    )
 
 
 def communicate(rows, cols, count, v, vp, coupling, tiles):
@@ -347,19 +390,14 @@
             pltpu.VMEM((2, T, T), F32),
             pltpu.VMEM(pair, BF16),
             pltpu.VMEM(pair, BF16),
-            pltpu.VMEM((2, 2 * T, T), F32),
-            pltpu.VMEM((2, SLOTS, 16, T), F32),
-            pltpu.VMEM((2, NY, 16, T), F32),
-            pltpu.VMEM((2, NX, 16, T), F32),
-            pltpu.VMEM((2, 16, T), F32),
-            pltpu.VMEM((2, 16, T), F32),
-            pltpu.VMEM((2, 16, T), F32),
-            pltpu.VMEM((2, 2 * T, T), F32),
+            pltpu.VMEM((2, T, T), BF16),
+            pltpu.VMEM((2, T, T), BF16),
             dma((2, 4, 2)), dma((2, 4, 2)), dma((NY, 2)), dma((NY, 2)),
-            dma((3, 2, 4)), dma((3, 2, 4)), dma((2, 4)), dma((2, 4)),
-            dma((2, SLOTS)), dma((2, SLOTS)), dma((2, NY)), dma((2, NY)),
-            dma((2, NX)), dma((2, NX)), dma((2, SLOTS)), dma((2, SLOTS)),
-        ],
+            dma((3, 2, 4)), dma((3, 2, 4)), dma((2, 4)), dma((2, 4)), dma((2,)), dma((2,)),
+        ]
+        + sum_scratch(T, NZ * NC, NX)
+        + sum_scratch(T, NX * NC, NZ)
+        + sum_scratch(2 * T, NZ * NC, NX),
         compiler_params=pltpu.CompilerParams(collective_id=0, has_side_effects=True),
         name="krylov_step",
     )(rows, cols, count, v, vp, coupling, tiles)

time: 88.5 us -> 85.1 us (0.962)
  Pallas kernels: 87 us -> 83.6 us
    pallas_call x1, Pallas kernels: 79 us -> 75.6 us  [communicate(): pl.pallas_call(step_kernel, out_shape=(jax.ShapeDtypeStruct((2 * T, T), F...]
where the time goes in v4:
time: 85.1 us; the launch traced here: 84.9 us
  Pallas kernels  83.6 us (98%)
  between operations  1.29 us (2%)
    pallas_call x1, Pallas kernels, communicate(): pl.pallas_call(step_kernel, out_shape=(jax.ShapeDtypeStruct((2 * T, T), F...  75.6 us
    pallas_call x1, Pallas kernels, factor(): pl.pallas_call(functools.partial(factor_kernel, total), out_shape=(jax.Sh...  7.99 us

profile of v4, /device:TPU:1, one launch (start us, length us, event | category | flops | bytes accessed | tf_op | source)
XLA Modules:
  0.0 84.9 jit_solution(11640546700633200223)
XLA Ops:
  1.3 75.6 %krylov_step.1 = (f32[256,128]{1,0:T(8,128)}, f32[256,128]{1,0:T(8,128)}, f32[256,128]{1,0:T(8,128)}) custom-call(s32[16]{0:T(128)} %bitcast.6, s32[16]{0:T(128)} %bitcast.7, s32[1]{0:T(128)} %bitcast.4.count_ref, f32[256,128]{1,0:T(8,128)} %v_ref.3, f32[256,128]{1,0:T(8,128)} %vp_ref.1, f32[128,128]{1,0:T(8,128)} %coupling_ref.1, bf16[16,128,128]{2,1,0:T(8,128)(2,1)} %bitcast.5), custom_call_target="tpu_custom_call" | custom-call | tf_op jit(solution)/shard_map/krylov_step/pallas_call | solution.py:364
  76.9 8.0 %factor.1 = (f32[256,128]{1,0:T(8,128)}, f32[128,128]{1,0:T(8,128)}, f32[128,128]{1,0:T(8,128)}) custom-call(f32[256,128]{1,0:T(8,128)} %get-tuple-element.6.late_ref, f32[256,128]{1,0:T(8,128)} %get-tuple-element.7.early_ref, f32[256,128]{1,0:T(8,128)} %get-tuple-element.8.open_ref, f32[256,128]{1,0:T(8,128)} %v_ref.3), custom_call_target="tpu_custom_call" | custom-call | tf_op jit(solution)/shard_map/factor/pallas_call | solution.py:471

commit v5 on v4

--- a/solution.py
+++ b/solution.py
@@ -67,12 +67,11 @@
     half[...] = v_s[...].astype(BF16).reshape(2, T, T)
     pl.semaphore_wait(barrier, len(peers))
 
-    pending = []
-
     def start(c):
         c.start()
-        pending.append(c)
-        return c
+
+    def sent(ref, sem):
+        copy(ref, ref, sem, sem, at(dc=1)).wait_send()
 
     def block(origin, h, c):
         return gathered.at[2 * (NC * origin + c) + h]
@@ -84,25 +83,18 @@
         else:
             dst = block((y - 2 * direction + NY) % NY, h, core)
             src, device = dst, at(dy=(far - 2) * direction)
-        return copy(src, dst, ring_s.at[d, far - 1, h], ring_r.at[d, far - 1, h], device)
+        return copy(src, dst, ring_s.at[0], ring_r.at[d, far - 1, h], device)
 
     def arrived(direction, far, h):
         d = 0 if direction == 1 else 1
         dst = block((y - direction * far + NY) % NY, h, core)
-        return copy(dst, dst, ring_s.at[d, far - 1, h], ring_r.at[d, far - 1, h], at(dy=direction))
+        return copy(dst, dst, ring_s.at[0], ring_r.at[d, far - 1, h], at(dy=direction))
 
     def to_pair(delta, h):
         origin = (y + delta + NY) % NY
         dst = block(origin, h, core)
         src = half.at[h] if delta == 0 else dst
-        k = (delta + NY) % NY
-        return copy(src, dst, pair_s.at[k, h], pair_r.at[k, h], at(dc=1))
-
-    def from_pair(delta, h):
-        origin = (y + delta + NY) % NY
-        dst = block(origin, h, 1 - core)
-        k = (delta + NY) % NY
-        return copy(dst, dst, pair_s.at[k, h], pair_r.at[k, h], at(dc=1))
+        return copy(src, dst, pair_s.at[0], pair_r.at[0], at(dc=1))
 
     def has(direction, far, h):
         return far < 4 or (h == 0) == (direction == 1)
@@ -117,7 +109,7 @@
     class Sum:
         def __init__(self, refs, over_z):
             self.part, self.totals, self.red, self.piece, self.send, self.recv = (
-                refs[0], refs[1], refs[2:5], refs[5:8], refs[8:12], refs[12:16]
+                refs[0], refs[1], refs[2:5], refs[5:8], refs[8], refs[9]
             )
             self.over_z = over_z
             self.place = (z if over_z else x) * NC + core
@@ -133,50 +125,56 @@
         def rows(self, ref, h):
             return ref.at[pl.ds(self.size * h, self.size)]
 
-        def move(self, stage, d, src, dst, device):
-            return copy(src, dst, self.send[stage].at[d], self.recv[stage].at[d], device)
+        def move(self, stage, src, dst, device):
+            return copy(src, dst, self.send.at[stage], self.recv.at[stage], device)
+
+        def others(self, stage):
+            if stage == 3:
+                return self.totals.at[pl.ds(0, self.size * (self.group - 1))]
+            return self.red[stage].at[pl.ds(0, self.red[stage].shape[0] - 1)]
+
+        def wait(self, stage):
+            self.move(stage, self.others(stage), self.others(stage), at(dc=1)).wait_recv()
+
+        def drain(self, stages):
+            for stage in stages:
+                self.move(stage, self.others(stage), self.others(stage), at(dc=1)).wait_send()
 
         def scatter(self):
             for d in range(1, self.group):
                 h, device = self.member(d)
-                start(self.move(0, d, self.rows(self.part, h), self.red[0].at[self.place], device))
+                start(self.move(0, self.rows(self.part, h), self.red[0].at[self.place], device))
             self.red[0][self.place] = self.part[pl.ds(self.size * self.place, self.size)]
 
-        def reduce(self, stage, i):
-            red, piece = self.red[stage], self.piece[stage]
-            n = red.shape[0]
-            for d in range(1, n):
-                slot = red.at[(i + n - d) % n]
-                self.move(stage, d, slot, slot, at(dc=1)).wait_recv()
-            piece[...] = jnp.sum(red[...], axis=0)
-            return piece
+        def reduce(self, stage):
+            self.wait(stage)
+            self.piece[stage][...] = jnp.sum(self.red[stage][...], axis=0)
+            return self.piece[stage]
 
         def spread(self, stage, piece, i, device_at):
             red = self.red[stage]
             for d in range(1, red.shape[0]):
-                start(self.move(stage, d, piece, red.at[i], device_at(d)))
+                start(self.move(stage, piece, red.at[i], device_at(d)))
             red[i] = piece[...]
 
         def over_y(self):
-            self.spread(1, self.reduce(0, self.place), y, lambda d: at(dy=d))
+            self.spread(1, self.reduce(0), y, lambda d: at(dy=d))
 
         def over_last(self):
-            piece = self.reduce(1, y)
+            piece = self.reduce(1)
             self.spread(2, piece, self.last, (lambda d: at(dx=d)) if self.over_z else (lambda d: at(dz=d)))
 
         def back(self):
-            piece = self.reduce(2, self.last)
+            piece = self.reduce(2)
             for d in range(1, self.group):
                 h, device = self.member(d)
-                start(self.move(3, d, piece, self.rows(self.totals, self.place), device))
+                start(self.move(3, piece, self.rows(self.totals, self.place), device))
             self.totals[pl.ds(self.size * self.place, self.size)] = piece[...]
 
         def collect(self):
-            for d in range(1, self.group):
-                slot = self.rows(self.totals, (self.place + self.group - d) % self.group)
-                self.move(3, d, slot, slot, at(dc=1)).wait_recv()
-
-    image, square, early = (Sum(sum_refs[16 * i : 16 * i + 16], over_z) for i, over_z in enumerate((True, False, True)))
+            self.wait(3)
+
+    image, square, early = (Sum(sum_refs[10 * i : 10 * i + 10], over_z) for i, over_z in enumerate((True, False, True)))
 
     def take(far):
         for h in range(2):
@@ -225,9 +223,8 @@
     early.over_y()
     take(3)
     take(4)
-    for delta in range(NY):
-        for h in range(2):
-            from_pair(delta, h).wait_recv()
+    others = gathered.at[pl.ds(0, SLOTS)]
+    copy(others, others, pair_s.at[0], pair_r.at[0], at(dc=1)).wait_recv()
 
     for t in range(SLOTS):
         value = sums[before[t]] + jnp.dot(tiles_s[t], gathered[cols_ref[t]], preferred_element_type=F32)
@@ -244,7 +241,7 @@
     def xcopy(kind, s, k):
         src = (fwd, direct, comb)[kind].at[s, k]
         dst = (fwd_in, direct_in, comb_in)[kind].at[s, k]
-        return copy(src, dst, x_s.at[kind, s, k], x_r.at[kind, s, k], at(dx=1 if s == 0 else -1))
+        return copy(src, dst, x_s.at[kind], x_r.at[kind, s, k], at(dx=1 if s == 0 else -1))
 
     side = (AHEAD, BEHIND)
 
@@ -267,10 +264,10 @@
             start(xcopy(2, s, k))
 
     def zcopy(s, k):
-        return copy(zsend.at[s, k], zrecv.at[s, k], z_s.at[s, k], z_r.at[s, k], at(dz=side[s][k]))
+        return copy(zsend.at[4 * s + k], zrecv.at[s, k], z_s.at[0], z_r.at[s, k], at(dz=side[s][k]))
 
     def zhalf_copy(s):
-        return copy(zhalf.at[s], zhalf_in.at[s], zh_s.at[s], zh_r.at[s], at(dz=1 if s == 0 else -1))
+        return copy(zhalf.at[s], zhalf_in.at[s], zh_s.at[0], zh_r.at[s], at(dz=1 if s == 0 else -1))
 
     def line_sum(s, k, h):
         mine = sums[latest[tile_of(0, side[s][k], h)]]
@@ -292,7 +289,7 @@
                 else:
                     if k == 1 and h == s:
                         value = value + zhalf_in[s].astype(F32)
-                    zsend[s, k, h] = value.astype(BF16)
+                    zsend[4 * s + k, h] = value.astype(BF16)
             if k > 0:
                 start(zcopy(s, k))
 
@@ -327,7 +324,14 @@
     square.part[...] = dot(opened, opened, ((0,), (0,)))
     square.scatter()
     open_ref[...] = opened
+    sent(gathered.at[pl.ds(0, 14)], ring_s.at[0])
+    sent(others, pair_s.at[0])
+    for kind, ref in enumerate((fwd, direct, comb)):
+        sent(ref, x_s.at[kind])
+    sent(zsend.at[pl.ds(0, 6)], z_s.at[0])
+    sent(zhalf, zh_s.at[0])
     early.collect()
+    early.drain(range(4))
     early_ref[...] = early.totals[...]
     square.over_y()
     image.over_y()
@@ -335,24 +339,25 @@
     image.over_last()
     image.back()
     square.back()
+    image.drain(range(3))
+    square.drain(range(3))
     image.collect()
     square.collect()
     late_ref[0:T] = image.totals[...]
     late_ref[T : 2 * T] = square.totals[...]
 
-    for c in pending:
-        c.wait_send()
+    image.drain((3,))
+    square.drain((3,))
 
 
 def sum_scratch(rows, group, last):
     size = rows // group
     counts = (group, NY, last)
-    sems = [pltpu.SemaphoreType.DMA((n,)) for n in counts + (group,)]
     return (
         [pltpu.VMEM((rows, T), F32)] * 2
         + [pltpu.VMEM((n, size, T), F32) for n in counts]
         + [pltpu.VMEM((size, T), F32)] * 3
-        + sems * 2
+        + [pltpu.SemaphoreType.DMA((4,))] * 2
     )
 
 
@@ -388,12 +393,12 @@
         + [pltpu.VMEM(pair, BF16)] * 6
         + [
             pltpu.VMEM((2, T, T), F32),
-            pltpu.VMEM(pair, BF16),
+            pltpu.VMEM((8, 2, T, T), BF16),
             pltpu.VMEM(pair, BF16),
             pltpu.VMEM((2, T, T), BF16),
             pltpu.VMEM((2, T, T), BF16),
-            dma((2, 4, 2)), dma((2, 4, 2)), dma((NY, 2)), dma((NY, 2)),
-            dma((3, 2, 4)), dma((3, 2, 4)), dma((2, 4)), dma((2, 4)), dma((2,)), dma((2,)),
+            dma((1,)), dma((2, 4, 2)), dma((1,)), dma((1,)),
+            dma((3,)), dma((3, 2, 4)), dma((1,)), dma((2, 4)), dma((1,)), dma((2,)),
         ]
         + sum_scratch(T, NZ * NC, NX)
         + sum_scratch(T, NX * NC, NZ)
@@ -422,47 +427,50 @@
     def spread(row):
         return jnp.broadcast_to(row, (8, T))
 
+    def mix(rows, weight):
+        value = None
+        for j in range(8):
+            term = weight[j] * rows[j]
+            value = term if value is None else value + term
+        return value
+
     for p in range(groups):
         panel, other = left[p], right[p]
         columns = [jnp.broadcast_to(panel[:, 8 * p + j : 8 * p + j + 1], (8, T)) for j in range(8)]
         a = [[spread(columns[j][i : i + 1]) for j in range(i + 1)] for i in range(8)]
-        inv = [[None] * 8 for _ in range(8)]
         low = [[None] * 8 for _ in range(8)]
+        inv = [None] * 8
+        rows_l = [spread(panel[j : j + 1]) for j in range(8)]
+        rows_r = [spread(other[j : j + 1]) for j in range(8)]
         for j in range(8):
-            inv[j][j] = lax.rsqrt(a[j][j])
+            inv[j] = lax.rsqrt(a[j][j])
             for i in range(j + 1, 8):
-                low[i][j] = a[i][j] * inv[j][j]
+                low[i][j] = a[i][j] * inv[j]
             for i in range(j + 1, 8):
                 for k in range(j + 1, i + 1):
                     a[i][k] = a[i][k] - low[i][j] * low[k][j]
-            for k in range(j):
-                s = low[j][k] * inv[k][k]
-                for m in range(k + 1, j):
-                    s = s + low[j][m] * inv[m][k]
-                inv[j][k] = -(s * inv[j][j])
-        rows_l = [spread(panel[j : j + 1]) for j in range(8)]
-        rows_r = [spread(other[j : j + 1]) for j in range(8)]
-
-        def mix(rows, weight, picks):
-            value = None
-            for j in picks:
-                term = weight(j) * rows[j]
-                value = term if value is None else value + term
-            return value
-
-        out_l = [mix(rows_l, lambda j, i=i: inv[i][j], range(i + 1)) for i in range(8)]
-        out_r = [mix(rows_r, lambda j, i=i: inv[i][j], range(i + 1)) for i in range(8)]
+            rows_l[j] = rows_l[j] * inv[j]
+            rows_r[j] = rows_r[j] * inv[j]
+            for i in range(j + 1, 8):
+                rows_l[i] = rows_l[i] - low[i][j] * rows_l[j]
+                rows_r[i] = rows_r[i] - low[i][j] * rows_r[j]
         for i in range(8):
             r = 8 * p + i
-            rfactor_ref[pl.ds(r, 1)] = jnp.where(lane >= r, out_l[i][0:1], 0.0)
-            inverse_ref[pl.ds(r, 1)] = out_r[i][0:1]
+            rfactor_ref[pl.ds(r, 1)] = jnp.where(lane >= r, rows_l[i][0:1], 0.0)
+            inverse_ref[pl.ds(r, 1)] = rows_r[i][0:1]
         if p + 1 < groups:
-            back_l = [mix(out_l, lambda i, j=j: inv[i][j], range(j, 8)) for j in range(8)]
-            back_r = [mix(out_r, lambda i, j=j: inv[i][j], range(j, 8)) for j in range(8)]
+            back_l, back_r = [None] * 8, [None] * 8
+            for j in range(7, -1, -1):
+                sum_l, sum_r = rows_l[j], rows_r[j]
+                for i in range(j + 1, 8):
+                    sum_l = sum_l - low[i][j] * back_l[i]
+                    sum_r = sum_r - low[i][j] * back_r[i]
+                back_l[j] = sum_l * inv[j]
+                back_r[j] = sum_r * inv[j]
             for g in range(p + 1, groups):
                 cols = [jnp.broadcast_to(left[g][:, 8 * p + j : 8 * p + j + 1], (8, T)) for j in range(8)]
-                left[g] = left[g] - mix(back_l, lambda j: cols[j], range(8))
-                right[g] = right[g] - mix(back_r, lambda j: cols[j], range(8))
+                left[g] = left[g] - mix(back_l, cols)
+                right[g] = right[g] - mix(back_r, cols)
     basis_ref[...] = dot(residual[...], inverse_ref[...], ((1,), (1,)))
 
 

time: 85.1 us -> 82.5 us (0.969)
  Pallas kernels: 83.6 us -> 81 us
    pallas_call x1, Pallas kernels: 75.6 us -> 72.6 us  [communicate(): pl.pallas_call(step_kernel, out_shape=(jax.ShapeDtypeStruct((2 * T, T), F...]
where the time goes in v5:
time: 82.5 us; the launch traced here: 82.2 us
  Pallas kernels  81 us (98%)
  between operations  1.29 us (2%)
    pallas_call x1, Pallas kernels, communicate(): pl.pallas_call(step_kernel, out_shape=(jax.ShapeDtypeStruct((2 * T, T), F...  72.6 us
    pallas_call x1, Pallas kernels, factor(): pl.pallas_call(functools.partial(factor_kernel, total), out_shape=(jax.Sh...  8.33 us

profile of v5, /device:TPU:1, one launch (start us, length us, event | category | flops | bytes accessed | tf_op | source)
XLA Modules:
  0.0 82.2 jit_solution(16755621164886037739)
XLA Ops:
  1.3 72.6 %krylov_step.1 = (f32[256,128]{1,0:T(8,128)}, f32[256,128]{1,0:T(8,128)}, f32[256,128]{1,0:T(8,128)}) custom-call(s32[16]{0:T(128)} %bitcast.6, s32[16]{0:T(128)} %bitcast.7, s32[1]{0:T(128)} %bitcast.4.count_ref, f32[256,128]{1,0:T(8,128)} %v_ref.3, f32[256,128]{1,0:T(8,128)} %vp_ref.1, f32[128,128]{1,0:T(8,128)} %coupling_ref.1, bf16[16,128,128]{2,1,0:T(8,128)(2,1)} %bitcast.5), custom_call_target="tpu_custom_call" | custom-call | tf_op jit(solution)/shard_map/krylov_step/pallas_call | solution.py:369
  73.9 8.3 %factor.1 = (f32[256,128]{1,0:T(8,128)}, f32[128,128]{1,0:T(8,128)}, f32[128,128]{1,0:T(8,128)}) custom-call(f32[256,128]{1,0:T(8,128)} %get-tuple-element.6.late_ref, f32[256,128]{1,0:T(8,128)} %get-tuple-element.7.early_ref, f32[256,128]{1,0:T(8,128)} %get-tuple-element.8.open_ref, f32[256,128]{1,0:T(8,128)} %v_ref.3), custom_call_target="tpu_custom_call" | custom-call | tf_op jit(solution)/shard_map/factor/pallas_call | solution.py:479

commit v6 on v5

--- a/solution.py
+++ b/solution.py
@@ -24,9 +24,9 @@
 
 
 def step_kernel(
-    rows_ref, cols_ref, count_ref, v_ref, vp_ref, coupling_ref, tiles_ref,
+    rows_in, cols_in, count_in, v_ref, vp_ref, coupling_ref, tiles_ref,
     open_ref, late_ref, early_ref,
-    v_s, vp_s, coupling_s, tiles_s, local_sem,
+    rows_ref, cols_ref, count_ref, v_s, vp_s, coupling_s, tiles_s, local_sem,
     latest, before, half, gathered, sums, sums16, prev_part, vt,
     fwd, direct, comb, fwd_in, direct_in, comb_in,
     own, zsend, zrecv, zhalf, zhalf_in,
@@ -49,20 +49,23 @@
             src_ref=src, dst_ref=dst, send_sem=send, recv_sem=recv, device_id=device, device_id_type=MESH
         )
 
-    barrier = pltpu.get_barrier_semaphore()
-    peers = [at(dz=d // 2, dc=d % 2) for d in range(1, 16)]
-    peers += [at(dy=d) for d in range(1, NY)] + [at(dx=d, dc=c) for d in range(1, NX) for c in range(2)]
-    for peer in peers:
-        pl.semaphore_signal(barrier, inc=1, device_id=peer, device_id_type=MESH)
-
     loads = [
         pltpu.make_async_copy(src, dst, local_sem.at[i])
         for i, (src, dst) in enumerate(
-            ((v_ref, v_s), (vp_ref, vp_s), (coupling_ref, coupling_s), (tiles_ref, tiles_s))
+            (
+                (v_ref, v_s), (vp_ref, vp_s), (coupling_ref, coupling_s), (tiles_ref, tiles_s),
+                (rows_in, rows_ref), (cols_in, cols_ref), (count_in, count_ref),
+            )
         )
     ]
     for load in loads:
         load.start()
+    barrier = pltpu.get_barrier_semaphore()
+    peers = [at(dy=d) for d in range(1, NY)] + [at(dz=d // 2, dc=d % 2) for d in range(1, 16)]
+    peers += [at(dx=d, dc=c) for d in range(1, NX) for c in range(2)]
+    for peer in peers:
+        pl.semaphore_signal(barrier, inc=1, device_id=peer, device_id_type=MESH)
+
     loads[0].wait()
     half[...] = v_s[...].astype(BF16).reshape(2, T, T)
     pl.semaphore_wait(barrier, len(peers))
@@ -203,6 +206,8 @@
 
     sums[SLOTS] = jnp.zeros((T, T), F32)
     sums16[SLOTS] = jnp.zeros((T, T), BF16)
+    for load in loads[4:]:
+        load.wait()
     count = count_ref[0]
     used = [jnp.where(t < count, rows_ref[t], -1) for t in range(SLOTS)]
 
@@ -363,7 +368,6 @@
 
 def communicate(rows, cols, count, v, vp, coupling, tiles):
     vmem = pl.BlockSpec(memory_space=pltpu.VMEM)
-    smem = pl.BlockSpec(memory_space=pltpu.SMEM)
     dma = pltpu.SemaphoreType.DMA
     pair = (2, 4, 2, T, T)
     return pl.pallas_call(
@@ -373,14 +377,17 @@
             jax.ShapeDtypeStruct((2 * T, T), F32),
             jax.ShapeDtypeStruct((2 * T, T), F32),
         ),
-        in_specs=[smem, smem, smem] + [pl.BlockSpec(memory_space=pl.ANY)] * 4,
+        in_specs=[pl.BlockSpec(memory_space=pl.ANY)] * 7,
         out_specs=(vmem, vmem, vmem),
         scratch_shapes=[
+            pltpu.SMEM((SLOTS,), jnp.int32),
+            pltpu.SMEM((SLOTS,), jnp.int32),
+            pltpu.SMEM((1,), jnp.int32),
             pltpu.VMEM((2 * T, T), F32),
             pltpu.VMEM((2 * T, T), F32),
             pltpu.VMEM((T, T), F32),
             pltpu.VMEM((SLOTS, T, T), BF16),
-            dma((4,)),
+            dma((7,)),
             pltpu.SMEM((NX * NZ * 2,), jnp.int32),
             pltpu.SMEM((SLOTS,), jnp.int32),
             pltpu.VMEM((2, T, T), BF16),

time: 82.5 us -> 81.8 us (level)
  no operation moved by 1% of the time
where the time goes in v6:
time: 81.8 us; the launch traced here: 81.7 us
  Pallas kernels  80.4 us (98%)
  between operations  1.29 us (2%)
    pallas_call x1, Pallas kernels, communicate(): pl.pallas_call(step_kernel, out_shape=(jax.ShapeDtypeStruct((2 * T, T), F...  72.1 us
    pallas_call x1, Pallas kernels, factor(): pl.pallas_call(functools.partial(factor_kernel, total), out_shape=(jax.Sh...  8.33 us

profile of v6, /device:TPU:1, one launch (start us, length us, event | category | flops | bytes accessed | tf_op | source)
XLA Modules:
  0.0 81.7 jit_solution(17519839724169881682)
XLA Ops:
  1.3 72.1 %krylov_step.1 = (f32[256,128]{1,0:T(8,128)}, f32[256,128]{1,0:T(8,128)}, f32[256,128]{1,0:T(8,128)}) custom-call(s32[16]{0:T(128)} %bitcast.6, s32[16]{0:T(128)} %bitcast.7, s32[1]{0:T(128)} %bitcast.4.count_in, f32[256,128]{1,0:T(8,128)} %v_ref.3, f32[256,128]{1,0:T(8,128)} %vp_ref.1, f32[128,128]{1,0:T(8,128)} %coupling_ref.1, bf16[16,128,128]{2,1,0:T(8,128)(2,1)} %bitcast.5), custom_call_target="tpu_custom_call" | custom-call | tf_op jit(solution)/shard_map/krylov_step/pallas_call | solution.py:373
  73.3 8.3 %factor.1 = (f32[256,128]{1,0:T(8,128)}, f32[128,128]{1,0:T(8,128)}, f32[128,128]{1,0:T(8,128)}) custom-call(f32[256,128]{1,0:T(8,128)} %get-tuple-element.6.late_ref, f32[256,128]{1,0:T(8,128)} %get-tuple-element.7.early_ref, f32[256,128]{1,0:T(8,128)} %get-tuple-element.8.open_ref, f32[256,128]{1,0:T(8,128)} %v_ref.3), custom_call_target="tpu_custom_call" | custom-call | tf_op jit(solution)/shard_map/factor/pallas_call | solution.py:486
